TPU v7x, 32 devices: a whole 2x2x4 slice. The times are simulated.
32 devices in a mesh: dp: 16 (over z, x, core), tensor: 2 (over y).
Axes of the slice: x: 2, y: 2, z: 4, core: 2. Of those that a mesh axis runs over, the one named last changes fastest.
Arguments:
- inputs: bfloat16 [16384, 1024], P(('dp', 'tensor')), may hold values from -6 to 6
- lengths: int32 [32], P('dp'), may hold values from 128 to 512, as said below
- w_qkv: bfloat16 [1024, 3, 1024], P(None, None, 'tensor'), may hold values from -0.1875 to 0.1875
- b_qv: bfloat16 [2, 1024], P(None, 'tensor'), may hold values from -3 to 3
- w_out: bfloat16 [1024, 1024], P('tensor'), may hold values from -1.5 to 1.5
- b_out: bfloat16 [1024], replicated, may hold values from -3 to 3
- gain_one: bfloat16 [1024], replicated, may hold values from 0.5 to 1.5
- shift_one: bfloat16 [1024], replicated, may hold values from -3 to 3
- w_in: bfloat16 [1024, 4096], P(None, 'tensor'), may hold values from -0.1875 to 0.1875
- b_in: bfloat16 [4096], P('tensor'), may hold values from -3 to 3
- w_down: bfloat16 [4096, 1024], P('tensor'), may hold values from -0.09375 to 0.09375
- b_down: bfloat16 [1024], replicated, may hold values from -3 to 3
- gain_two: bfloat16 [1024], replicated, may hold values from 0.5 to 1.5
- shift_two: bfloat16 [1024], replicated, may hold values from -3 to 3
- cotangent: bfloat16 [16384, 1024], P(('dp', 'tensor')), may hold values from -6 to 6
Outputs:
- output: bfloat16 [16384, 1024], P(('dp', 'tensor'))
- grad_inputs: bfloat16 [16384, 1024], P(('dp', 'tensor'))
- grad_w_qkv: float32 [1024, 3, 1024], P(None, None, 'tensor')
- grad_b_qv: float32 [2, 1024], P(None, 'tensor')
- grad_w_out: float32 [1024, 1024], P('tensor')
- grad_b_out: float32 [1024], replicated
- grad_gain_one: float32 [1024], replicated
- grad_shift_one: float32 [1024], replicated
- grad_w_in: float32 [1024, 4096], P(None, 'tensor')
- grad_b_in: float32 [4096], P('tensor')
- grad_w_down: float32 [4096, 1024], P('tensor')
- grad_b_down: float32 [1024], replicated
- grad_gain_two: float32 [1024], replicated
- grad_shift_two: float32 [1024], replicated
Inputs may be any that keep to these rules, and one draw needn't show every extreme that they name: `lengths`: each sequence's count of valid token slots; slots at or past it are padding. Some sequence has exactly 512 and some exactly 128.
All inputs are finite; a program needn't handle non-finite values.
Results may differ from a plain program's by a relative error of at most 0.02.
Values may be sent and summed in bfloat16 or wider, within the bound.
A program may use at most 128 MiB of HBM per device.

v0:
```python
import jax
import jax.numpy as jnp
from jax import lax
from jax.sharding import PartitionSpec as P

HEAD = 64
SEQ = 512
SEQ_DEV = 2


EPSILON = 1e-12
NEG_FILL = -1000000000.0


def gelu_exact(values):
    return jax.nn.gelu(values, approximate=False)


def norm_forward(values, gain_vec, shift_vec):
    center = values - jnp.mean(values, axis=-1, keepdims=True)
    spread = jnp.mean(center * center, axis=-1, keepdims=True)
    inverse = lax.rsqrt(spread + EPSILON)
    scaled = center * inverse
    return (scaled * gain_vec + shift_vec, scaled, inverse)


def norm_backward(grad_out, scaled, inverse, gain_vec):
    grad_scaled = grad_out * gain_vec
    mean_one = jnp.mean(grad_scaled, axis=-1, keepdims=True)
    mean_two = jnp.mean(grad_scaled * scaled, axis=-1, keepdims=True)
    grad_in = inverse * (grad_scaled - mean_one - scaled * mean_two)
    return (grad_in, jnp.sum(grad_out * scaled, axis=0), jnp.sum(grad_out, axis=0))


def masked_scores(queries, key_rows, length):
    score_scale = HEAD ** (-0.5)
    scores = (
        jnp.einsum("qhe,khe->hqk", queries, key_rows, preferred_element_type=jnp.float32)
        * score_scale
    )
    key_valid = (jnp.arange(SEQ) < length)[None, None, :]
    return jnp.where(key_valid, scores, NEG_FILL)


def attend_forward(element):
    queries, key_rows, value_rows, length = element
    scores = masked_scores(queries, key_rows, length)
    peak_score = jnp.max(scores, axis=-1, keepdims=True)
    shifted_exp = jnp.exp(scores - peak_score)
    denominator = jnp.sum(shifted_exp, axis=-1, keepdims=True)
    probability = (shifted_exp / denominator).astype(jnp.bfloat16)
    context = jnp.einsum(
        "hqk,khe->qhe", probability, value_rows, preferred_element_type=jnp.float32
    )
    return (context.astype(jnp.bfloat16), (peak_score + jnp.log(denominator))[..., 0])


def attend_backward(element):
    queries, key_rows, value_rows, length, log_total, grad_context = element
    score_scale = HEAD ** (-0.5)
    scores = masked_scores(queries, key_rows, length)
    probability = jnp.exp(scores - log_total[..., None])
    grad_prob = jnp.einsum(
        "qhe,khe->hqk", grad_context, value_rows, preferred_element_type=jnp.float32
    )
    grad_value = jnp.einsum(
        "hqk,qhe->khe",
        probability.astype(jnp.bfloat16),
        grad_context,
        preferred_element_type=jnp.float32,
    )
    grad_scores = probability * (
        grad_prob - jnp.sum(probability * grad_prob, axis=-1, keepdims=True)
    )
    grad_scores = grad_scores.astype(jnp.bfloat16)
    grad_query = (
        jnp.einsum("hqk,khe->qhe", grad_scores, key_rows, preferred_element_type=jnp.float32)
        * score_scale
    )
    grad_key = (
        jnp.einsum("hqk,qhe->khe", grad_scores, queries, preferred_element_type=jnp.float32)
        * score_scale
    )
    return jnp.stack([grad_query, grad_key, grad_value], axis=1).astype(jnp.bfloat16)


def row_mask(lengths, rows_dev):
    places = lax.axis_index("tensor") * rows_dev + jnp.arange(rows_dev)
    sequence_of = places // SEQ
    offset = places % SEQ
    matches = sequence_of[:, None] == jnp.arange(lengths.shape[0])[None, :]
    limit_rows = jnp.sum(jnp.where(matches, lengths[None, :], 0), axis=1)
    return (offset < limit_rows).astype(jnp.float32)[:, None]


def forward_pass(inputs, lengths, weights):
    (
        w_qkv,
        b_qv,
        w_out,
        b_out,
        gain_one,
        shift_one,
        w_in,
        b_in,
        w_down,
        b_down,
        gain_two,
        shift_two,
    ) = weights
    width_dev = w_qkv.shape[2]
    gathered = lax.all_gather(inputs, "tensor", axis=0, tiled=True)
    bias_three = jnp.stack([b_qv[0], jnp.zeros_like(b_qv[0]), b_qv[1]]).astype(jnp.float32)
    projected = (
        jnp.einsum("td,dcf->tcf", gathered, w_qkv, preferred_element_type=jnp.float32) + bias_three
    ).astype(jnp.bfloat16)
    shaped = projected.reshape(SEQ_DEV, SEQ, 3, width_dev // HEAD, HEAD)
    context, log_total = lax.map(
        attend_forward, (shaped[:, :, 0], shaped[:, :, 1], shaped[:, :, 2], lengths)
    )
    context = context.reshape(SEQ_DEV * SEQ, width_dev)
    segment = context
    branch = lax.psum_scatter(
        jnp.dot(segment, w_out, preferred_element_type=jnp.float32).astype(jnp.bfloat16),
        "tensor",
        scatter_dimension=0,
        tiled=True,
    ).astype(jnp.float32) + b_out.astype(jnp.float32)
    normed, scaled_one, inverse_one = norm_forward(
        inputs.astype(jnp.float32) + branch,
        gain_one.astype(jnp.float32),
        shift_one.astype(jnp.float32),
    )
    normed_all = lax.all_gather(normed.astype(jnp.bfloat16), "tensor", axis=0, tiled=True)
    hidden = jnp.dot(normed_all, w_in, preferred_element_type=jnp.float32) + b_in.astype(
        jnp.float32
    )
    active = gelu_exact(hidden).astype(jnp.bfloat16)
    segment = active
    second = lax.psum_scatter(
        jnp.dot(segment, w_down, preferred_element_type=jnp.float32).astype(jnp.bfloat16),
        "tensor",
        scatter_dimension=0,
        tiled=True,
    ).astype(jnp.float32) + b_down.astype(jnp.float32)
    output, scaled_two, inverse_two = norm_forward(
        normed + second, gain_two.astype(jnp.float32), shift_two.astype(jnp.float32)
    )
    return (
        gathered,
        projected,
        context,
        log_total,
        scaled_one,
        inverse_one,
        normed_all,
        hidden,
        active,
        scaled_two,
        inverse_two,
        output,
    )


def local(
    inputs,
    lengths,
    w_qkv,
    b_qv,
    w_out,
    b_out,
    gain_one,
    shift_one,
    w_in,
    b_in,
    w_down,
    b_down,
    gain_two,
    shift_two,
    cotangent,
):
    weights = (
        w_qkv,
        b_qv,
        w_out,
        b_out,
        gain_one,
        shift_one,
        w_in,
        b_in,
        w_down,
        b_down,
        gain_two,
        shift_two,
    )
    first_pass = forward_pass(inputs, lengths, weights)
    output = first_pass[11].astype(jnp.bfloat16)
    recorded = forward_pass(inputs, lengths, weights)
    (
        gathered,
        projected,
        context,
        log_total,
        scaled_one,
        inverse_one,
        normed_all,
        hidden,
        active,
        scaled_two,
        inverse_two,
        _,
    ) = recorded
    rows_dev = inputs.shape[0]
    width_dev = w_qkv.shape[2]
    grad_out = cotangent.astype(jnp.float32) * row_mask(lengths, rows_dev)
    grad_two, grad_gain_two, grad_shift_two = norm_backward(
        grad_out, scaled_two, inverse_two, gain_two.astype(jnp.float32)
    )
    grad_second = grad_two.astype(jnp.bfloat16)
    grad_b_down = jnp.sum(grad_second.astype(jnp.float32), axis=0)
    second_all = lax.all_gather(grad_second, "tensor", axis=0, tiled=True)
    grad_w_down = jnp.einsum("tf,td->fd", active, second_all, preferred_element_type=jnp.float32)
    grad_active = jnp.einsum("td,fd->tf", second_all, w_down, preferred_element_type=jnp.float32)
    _, gelu_pull = jax.vjp(gelu_exact, hidden)
    grad_hidden = gelu_pull(grad_active)[0].astype(jnp.bfloat16)
    grad_b_in = jnp.sum(grad_hidden.astype(jnp.float32), axis=0)
    grad_w_in = jnp.einsum("td,tf->df", normed_all, grad_hidden, preferred_element_type=jnp.float32)
    segment = grad_hidden
    grad_normed = grad_two + lax.psum_scatter(
        jnp.einsum("tf,df->td", segment, w_in, preferred_element_type=jnp.float32).astype(
            jnp.bfloat16
        ),
        "tensor",
        scatter_dimension=0,
        tiled=True,
    ).astype(jnp.float32)
    grad_first, grad_gain_one, grad_shift_one = norm_backward(
        grad_normed, scaled_one, inverse_one, gain_one.astype(jnp.float32)
    )
    grad_branch = grad_first.astype(jnp.bfloat16)
    grad_b_out = jnp.sum(grad_branch.astype(jnp.float32), axis=0)
    branch_all = lax.all_gather(grad_branch, "tensor", axis=0, tiled=True)
    grad_w_out = jnp.einsum("tf,td->fd", context, branch_all, preferred_element_type=jnp.float32)
    grad_context = jnp.einsum(
        "td,fd->tf", branch_all, w_out, preferred_element_type=jnp.float32
    ).astype(jnp.bfloat16)
    heads_dev = width_dev // HEAD
    shaped = projected.reshape(SEQ_DEV, SEQ, 3, heads_dev, HEAD)
    grad_shaped = grad_context.reshape(SEQ_DEV, SEQ, heads_dev, HEAD)
    grad_proj = lax.map(
        attend_backward,
        (shaped[:, :, 0], shaped[:, :, 1], shaped[:, :, 2], lengths, log_total, grad_shaped),
    )
    grad_proj = grad_proj.reshape(SEQ_DEV * SEQ, 3, width_dev)
    grad_w_qkv = jnp.einsum("td,tcf->dcf", gathered, grad_proj, preferred_element_type=jnp.float32)
    grad_b_qv = jnp.sum(grad_proj[:, 0::2].astype(jnp.float32), axis=0)
    segment = grad_proj
    grad_inputs = (
        grad_first
        + lax.psum_scatter(
            jnp.einsum("tcf,dcf->td", segment, w_qkv, preferred_element_type=jnp.float32).astype(
                jnp.bfloat16
            ),
            "tensor",
            scatter_dimension=0,
            tiled=True,
        ).astype(jnp.float32)
    ).astype(jnp.bfloat16)
    small_terms = jnp.stack(
        [grad_gain_one, grad_shift_one, grad_b_out, grad_gain_two, grad_shift_two, grad_b_down]
    )
    grad_w_qkv, grad_b_qv, grad_w_out, grad_w_in, grad_b_in, grad_w_down, small_terms = (
        lax.psum(grad_w_qkv.astype(jnp.bfloat16), "dp").astype(jnp.float32),
        lax.psum(grad_b_qv.astype(jnp.bfloat16), "dp").astype(jnp.float32),
        lax.psum(grad_w_out.astype(jnp.bfloat16), "dp").astype(jnp.float32),
        lax.psum(grad_w_in.astype(jnp.bfloat16), "dp").astype(jnp.float32),
        lax.psum(grad_b_in.astype(jnp.bfloat16), "dp").astype(jnp.float32),
        lax.psum(grad_w_down.astype(jnp.bfloat16), "dp").astype(jnp.float32),
        lax.psum(small_terms.astype(jnp.bfloat16), "dp").astype(jnp.float32),
    )
    small_sums = lax.psum(small_terms, "tensor")
    return (
        output,
        grad_inputs,
        grad_w_qkv,
        grad_b_qv,
        grad_w_out,
        small_sums[2],
        small_sums[0],
        small_sums[1],
        grad_w_in,
        grad_b_in,
        grad_w_down,
        small_sums[5],
        small_sums[3],
        small_sums[4],
    )


def solution(mesh):
    in_specs = (
        P(("dp", "tensor"), None),
        P("dp"),
        P(None, None, "tensor"),
        P(None, "tensor"),
        P("tensor", None),
        P(),
        P(),
        P(),
        P(None, "tensor"),
        P("tensor"),
        P("tensor", None),
        P(),
        P(),
        P(),
        P(("dp", "tensor"), None),
    )
    out_specs = (
        P(("dp", "tensor"), None),
        P(("dp", "tensor"), None),
        P(None, None, "tensor"),
        P(None, "tensor"),
        P("tensor", None),
        P(),
        P(),
        P(),
        P(None, "tensor"),
        P("tensor"),
        P("tensor", None),
        P(),
        P(),
        P(),
    )
    return jax.shard_map(local, mesh=mesh, in_specs=in_specs, out_specs=out_specs, check_vma=False)
```

profile of v0, /device:TPU:0, one launch (start us, length us, event | category | flops | bytes accessed | tf_op | source)
XLA Modules:
  0.0 821.6 jit_solution(8825793125772244201)
XLA Ops:
  8.9 36.5 %all-gather.6.cloned.1.call-done = bf16[1024,1024]{1,0:T(8,128)(2,1)} async-done(((bf16[512,1024]{1,0:T(8,128)(2,1)}), bf16[1024,1024]{1,0:T(8,128)(2,1)}) %all-gather.6.cloned.1.call-update) | async-done | bytes 2097168 | tf_op jit(solution)/shard_map/all_gather | solution.py:112
  45.4 6.3 add_convert_fusion.1
  71.3 18.9 %while.33 = (s32[]{:T(128)}, bf16[2,512,8,64]{1,3,2,0:T(8,128)(2,1)}, f32[2,8,512]{2,1,0:T(8,128)S(1)}, bf16[2,512,8,64]{1,3,2,0:T(8,128)(2,1)}, s32[2]{0:T(128)...) while((s32[]{:T(128)}, bf16[2,512,8,64]{1,3,2,0:T(8,128)(2,1)}, ...), condition=%wide.region_13.14_spmd, body=%wide.region_10.13_spmd.sunk | while | flops 562295296 | bytes 31592580 | solution.py:118
  97.8 28.8 %while.32 = (s32[]{:T(128)}, bf16[2,512,8,64]{1,3,2,0:T(8,128)(2,1)}, bf16[2,512,8,64]{1,3,2,0:T(8,128)(2,1)}, s32[2]{0:T(128)S(1)}, bf16[2,512,8,64]{1,3,2,0:T(...) while((s32[]{:T(128)}, bf16[2,512,8,64]{1,3,2,0:T(8,128)(2,1)}, bf16[2,512,8,64]{1,3,2,0:T(8,128)(2,1)}, ...), condition=%wide.region_3.4_spmd, body=%wide.region_0.3_spmd.sunk | while | flops 549716992 | bytes 18910300 | solution.py:118
  99.1 7.9 fusion.232
  113.4 7.9 fusion.232
  134.2 29.8 %reduce-scatter.7.cloned.1.call-done = bf16[512,1024]{1,0:T(8,128)(2,1)} async-done(((bf16[1024,1024]{1,0:T(8,128)(2,1)}), bf16[512,1024]{1,0:T(8,128)(2,1)}) %reduce-scatter.7.cloned.1.call-update) | async-done | bytes 1048592 | tf_op jit(solution)/shard_map/reduce_scatter | solution.py:123
  170.5 32.8 %all-gather.10.cloned.1.call-done = bf16[1024,1024]{1,0:T(8,128)(2,1)} async-done(((bf16[512,1024]{1,0:T(8,128)(2,1)}), bf16[1024,1024]{1,0:T(8,128)(2,1)}) %all-gather.10.cloned.1.call-update) | async-done | bytes 2097168 | tf_op jit(solution)/shard_map/all_gather | solution.py:134
  203.4 26.0 %multiply_convert_fusion.1 = (bf16[1024,2048]{1,0:T(8,128)(2,1)S(1)}, f32[1024,2048]{1,0:T(8,128)}, f32[1024,2048]{1,0:T(8,128)}) fusion(f32[2048]{0:T(1024)S(1)} %convert_element_type.208, bf16[1024,1024]{1,0:T(8,128)(2,1)} %all-gather.10.cloned.1.call-done, bf16[1024,2048]{1,0:T(8,128)(2,1)} %param.29), kind=kOutput, calls=%fused_computation.99 | convolution fusion | flops 4433379328 | bytes 27271168 | tf_op jit(solution)/shard_map/dot_general | solution.py:135
  237.2 31.8 %reduce-scatter.13.cloned.1.call-done = bf16[512,1024]{1,0:T(8,128)(2,1)} async-done(((bf16[1024,1024]{1,0:T(8,128)(2,1)}), bf16[512,1024]{1,0:T(8,128)(2,1)}) %reduce-scatter.13.cloned.1.call-update) | async-done | bytes 1048592 | tf_op jit(solution)/shard_map/reduce_scatter | solution.py:140
  277.2 33.0 %all-gather.12.cloned.1.call-done = bf16[1024,1024]{1,0:T(8,128)(2,1)} async-done(((bf16[512,1024]{1,0:T(8,128)(2,1)}), bf16[1024,1024]{1,0:T(8,128)(2,1)}) %all-gather.12.cloned.1.call-update) | async-done | bytes 2097168 | tf_op jit(solution)/shard_map/all_gather | solution.py:221
  310.3 14.0 %fusion.162 = (bf16[2048]{0:T(1024)(128)(2,1)}, bf16[1024,2048]{1,0:T(8,128)(2,1)S(1)}) fusion(f32[1024,2048]{1,0:T(8,128)} %get-tuple-element.295, f32[1024,2048]{1,0:T(8,128)} %get-tuple-element.313, f32[2048]{0:T(1024)S(1)} %convert_element_type.208, bf16[1024,1024]{1,0:T(8,128)(2,1)} %all-gather.12.cloned.1.call-done, bf16[2048,1024]{1,0:T(8,128)(2,1)} %param.31), kind=kOutput, calls=%fused_computation.236 | convolution fusion | flops 4328519680 | bytes 27275264 | tf_op jit(solution)/shard_map/td,fd->tf/dot_general | solution.py:223
  332.1 31.9 %reduce-scatter.15.cloned.1.call-done = bf16[512,1024]{1,0:T(8,128)(2,1)} async-done(((bf16[1024,1024]{1,0:T(8,128)(2,1)}), bf16[512,1024]{1,0:T(8,128)(2,1)}) %reduce-scatter.15.cloned.1.call-update) | async-done | bytes 1048592 | tf_op jit(solution)/shard_map/reduce_scatter | solution.py:229
  375.3 30.0 %all-gather.14.cloned.1.call-done = bf16[1024,1024]{1,0:T(8,128)(2,1)} async-done(((bf16[512,1024]{1,0:T(8,128)(2,1)}), bf16[1024,1024]{1,0:T(8,128)(2,1)}) %all-gather.14.cloned.1.call-update) | async-done | bytes 2097168 | tf_op jit(solution)/shard_map/all_gather | solution.py:242
  416.9 23.7 %all-gather.8.cloned.1.call-done = bf16[1024,1024]{1,0:T(8,128)(2,1)} async-done(((bf16[512,1024]{1,0:T(8,128)(2,1)}), bf16[1024,1024]{1,0:T(8,128)(2,1)}) %all-gather.8.cloned.1.call-update) | async-done | bytes 2097168 | tf_op jit(solution)/shard_map/all_gather | solution.py:134
  440.5 29.6 %fusion.118 = bf16[1024,1024]{1,0:T(8,128)(2,1)} fusion(bf16[2048,1024]{1,0:T(8,128)(2,1)} %param.31, f32[2048]{0:T(1024)S(1)} %convert_element_type.208, bf16[1024,1024]{1,0:T(8,128)(2,1)} %all-gather.8.cloned.1.call-done, bf16[1024,2048]{1,0:T(8,128)(2,1)} %param.29), kind=kOutput, calls=%fused_computation.163 | convolution fusion | flops 8729395200 | bytes 12591104 | tf_op jit(solution)/shard_map/dot_general | solution.py:141
  470.2 32.0 %while.34 = (s32[]{:T(128)}, bf16[2,512,3,8,64]{1,4,3,2,0:T(8,128)(2,1)}, bf16[2,512,8,64]{1,3,2,0:T(8,128)(2,1)}, s32[2]{0:T(128)S(1)}, bf16[2,512,8,64]{1,3,2,...) while((s32[]{:T(128)}, ...), condition=%wide.region_28.29_spmd, body=%wide.region_26.28_spmd.sunk | while | flops 1379660288 | bytes 88199920 | solution.py:250
  502.2 6.8 copy.81
  515.1 6.9 bitcast_convert_fusion
  522.0 9.6 %convolution_convert_fusion = bf16[2048,1024]{1,0:T(8,128)(2,1)} fusion(bf16[1024,2048]{1,0:T(8,128)(2,1)} %copy-done.55, bf16[1024,1024]{1,0:T(8,128)(2,1)} %all-gather.12.cloned.1.call-done), kind=kOutput, calls=%fused_computation.131 | convolution fusion | flops 4297064448 | bytes 10485760 | tf_op jit(solution)/shard_map/tf,td->fd/dot_general | solution.py:222
  548.4 63.7 %all-reduce = (bf16[6,1024]{1,0:T(8,128)(2,1)S(1)}, bf16[2,512]{1,0:T(2,128)(2,1)S(1)}, bf16[2048]{0:T(1024)(128)(2,1)S(1)}) all-reduce(bf16[6,1024]{1,0:T(8,128)(2,1)S(1)} %stack.54, bf16[2,512]{1,0:T(2,128)(2,1)S(1)} %slice_reduce_fusion, bf16[2048]{0:T(1024)(128)(2,1)S(1)} %copy-done.38), channel_id=1, replica_groups=mesh['dp'=16,'tensor'=2] {'dp'}, use_global_device_ids=true, to_apply=%region_40.41 | all-reduce | flops 9216 | bytes 36864 | tf_op jit(solution)/shard_map/psum | solution.py:279
  613.4 7.5 psum.60
  629.4 165.5 %all-reduce.4.cloned.1.call-done = (bf16[1024,3,512]{0,2,1:T(8,128)(2,1)}, bf16[512,1024]{1,0:T(8,128)(2,1)}, bf16[1024,2048]{1,0:T(8,128)(2,1)}, bf16[2048,1024]{1,0:T(8,128)(2,1)}) async-done(((bf16[1024,3,512]{0,2,1:T(8,128)(2,1)}, bf16[512,1024]{1,0:T(8,128)(2,1)}, bf16[1024,2048]{1,0:T(8,128)(2,1)}, bf16[2048,1024]{1,0:T(8,128)(2,1)}), (bf16[1024,3,512]{0,2,1:T(8,128)(2,1)}, ...) | async-done | bytes 12582928 | tf_op jit(solution)/shard_map/psum | solution.py:273
  794.9 6.8 convert_element_type.243
  (264 shorter events, 197.6 us)
Async XLA Ops:
  7.2 38.2 %all-gather.6.cloned.1.call-start = ((), (), s32[]{:S(2)}) async-start(), calls=%async_computation.6 | async-start | bytes 3145728 | tf_op jit(solution)/shard_map/all_gather | solution.py:112
  7.9 124.2 %reduce-scatter.11.cloned.1.call-start = ((), (), s32[]{:S(2)}) async-start(), calls=%async_computation.10 | async-start | bytes 3145728 | tf_op jit(solution)/shard_map/reduce_scatter | solution.py:123
  96.5 67.5 %reduce-scatter.7.cloned.1.call-start = ((), (), s32[]{:S(2)}) async-start(), calls=%async_computation.7 | async-start | bytes 3145728 | tf_op jit(solution)/shard_map/reduce_scatter | solution.py:123
  132.0 71.3 %all-gather.10.cloned.1.call-start = ((), (), s32[]{:S(2)}) async-start(), calls=%async_computation.11 | async-start | bytes 3145728 | tf_op jit(solution)/shard_map/all_gather | solution.py:134
  132.1 239.9 %copy-start.15 = (f32[1024]{0:T(1024)}, f32[1024]{0:T(1024)S(1)}, u32[]{:S(2)}) copy-start(f32[1024]{0:T(1024)S(1)} %convert_element_type.204) | copy-start | bytes 12292
  132.1 239.9 %copy-start.19 = (f32[1024]{0:T(1024)}, f32[1024]{0:T(1024)S(1)}, u32[]{:S(2)}) copy-start(f32[1024]{0:T(1024)S(1)} %convert_element_type.205) | copy-start | bytes 12292
  132.1 239.9 %copy-start.21 = (f32[1024]{0:T(1024)}, f32[1024]{0:T(1024)S(1)}, u32[]{:S(2)}) copy-start(f32[1024]{0:T(1024)S(1)} %convert_element_type.206) | copy-start | bytes 12292
  170.1 98.9 %reduce-scatter.13.cloned.1.call-start = ((), (), s32[]{:S(2)}) async-start(), calls=%async_computation.12 | async-start | bytes 3145728 | tf_op jit(solution)/shard_map/reduce_scatter | solution.py:140
  237.0 73.3 %all-gather.12.cloned.1.call-start = ((), (), s32[]{:S(2)}) async-start(), calls=%async_computation.13 | async-start | bytes 3145728 | tf_op jit(solution)/shard_map/all_gather | solution.py:221
  277.0 87.0 %reduce-scatter.15.cloned.1.call-start = ((), (), s32[]{:S(2)}) async-start(), calls=%async_computation.14 | async-start | bytes 3145728 | tf_op jit(solution)/shard_map/reduce_scatter | solution.py:229
  332.0 73.2 %all-gather.14.cloned.1.call-start = ((), (), s32[]{:S(2)}) async-start(), calls=%async_computation.15 | async-start | bytes 3145728 | tf_op jit(solution)/shard_map/all_gather | solution.py:242
  332.1 40.0 %copy-start.27 = (f32[512]{0:T(512)}, f32[512]{0:T(512)S(1)}, u32[]{:S(2)}) copy-start(f32[512]{0:T(512)S(1)} %broadcast_multiply_fusion.7) | copy-start | bytes 6148
  372.0 68.6 %all-gather.8.cloned.1.call-start = ((), (), s32[]{:S(2)}) async-start(), calls=%async_computation.8 | async-start | bytes 3145728 | tf_op jit(solution)/shard_map/all_gather | solution.py:134
  375.2 246.3 %reduce-scatter.9.cloned.1.call-start = ((), (), s32[]{:S(2)}) async-start(), calls=%async_computation.9 | async-start | bytes 3145728 | tf_op jit(solution)/shard_map/reduce_scatter | solution.py:140
  416.8 53.4 %copy-start.18 = (f32[2,8,512]{2,1,0:T(8,128)S(1)}, f32[2,8,512]{2,1,0:T(8,128)}, u32[]{:S(2)}) copy-start(f32[2,8,512]{2,1,0:T(8,128)} %copy-done.17) | copy-start | bytes 98308
  470.2 156.0 %reduce-scatter.17.cloned.1.call-start = ((), (), s32[]{:S(2)}) async-start(), calls=%async_computation.16 | async-start | bytes 3145728 | tf_op jit(solution)/shard_map/reduce_scatter | solution.py:260
  522.0 272.9 %all-reduce.4.cloned.1.call-start = ((), (), s32[]{:S(2)}) async-start(), calls=%async_computation.17 | async-start | bytes 25165824 | tf_op jit(solution)/shard_map/psum | solution.py:273
  545.7 75.8 %copy-start.16 = (f32[1024]{0:T(1024)S(1)}, f32[1024]{0:T(1024)}, u32[]{:S(2)}) copy-start(f32[1024]{0:T(1024)} %copy-done.15) | copy-start | bytes 12292
  545.7 75.8 %copy-start.20 = (f32[1024]{0:T(1024)S(1)}, f32[1024]{0:T(1024)}, u32[]{:S(2)}) copy-start(f32[1024]{0:T(1024)} %copy-done.19) | copy-start | bytes 12292
  545.7 75.8 %copy-start.22 = (f32[1024]{0:T(1024)S(1)}, f32[1024]{0:T(1024)}, u32[]{:S(2)}) copy-start(f32[1024]{0:T(1024)} %copy-done.21) | copy-start | bytes 12292
  545.7 75.8 %copy-start.26 = (f32[1024]{0:T(1024)S(1)}, f32[1024]{0:T(1024)}, u32[]{:S(2)}) copy-start(f32[1024]{0:T(1024)} %copy-done.25) | copy-start | bytes 12292
  545.7 75.8 %copy-start.28 = (f32[512]{0:T(512)S(1)}, f32[512]{0:T(512)}, u32[]{:S(2)}) copy-start(f32[512]{0:T(512)} %copy-done.27) | copy-start | bytes 6148
  545.7 75.8 %copy-start.30 = (f32[512]{0:T(512)S(1)}, f32[512]{0:T(512)}, u32[]{:S(2)}) copy-start(f32[512]{0:T(512)} %copy-done.29) | copy-start | bytes 6148
  548.4 76.4 %copy-start.24 = (f32[1024]{0:T(1024)S(1)}, f32[1024]{0:T(1024)}, u32[]{:S(2)}) copy-start(f32[1024]{0:T(1024)} %copy-done.23) | copy-start | bytes 12292
  (49 other events, 373.1 us)
Sparse Core Ops, SparseCore 0:
  9.6 35.8 all-gather.5
  96.6 31.8 reduce-scatter.10
  132.1 31.8 reduce-scatter.6
  170.2 33.1 all-gather.9
  237.1 31.8 reduce-scatter.12
  277.1 33.0 all-gather.11
  332.1 31.8 reduce-scatter.14
  372.1 33.1 all-gather.13
  407.4 33.1 all-gather.7
  470.3 31.8 reduce-scatter.8
  522.1 31.8 reduce-scatter.16
  559.5 235.3 all-reduce.3
where the time goes:
time: 831 us; the launch traced here: 822 us
  waiting for transfers between devices  416 us (50%)
  matrix products  185 us (22%)
  blocking collectives  71.2 us (9%)
  other arithmetic  68.3 us (8%)
  local copies, waits for them, and re-layouts  63.9 us (8%)
  between operations  15.3 us (2%)
    psum x1, waiting for transfers between devices, local(): lax.psum(grad_w_qkv.astype(jnp.bfloat16), 'dp').astype(jnp.float32)  165 us
    psum x1, blocking collectives, local(): lax.psum(small_terms.astype(jnp.bfloat16), 'dp').astype(jnp.float32)  63.7 us
    all_gather x2, waiting for transfers between devices, forward_pass(): lax.all_gather(normed.astype(jnp.bfloat16), 'tensor', axis=0, tiled=True)  56.5 us
    all_gather x1, waiting for transfers between devices, forward_pass(): gathered = lax.all_gather(inputs, 'tensor', axis=0, tiled=True)  36.5 us
    dot_general x2, matrix products, forward_pass(): jnp.dot(segment, w_down, preferred_element_type=jnp.float32)  35.3 us
    all_gather x1, waiting for transfers between devices, local(): second_all = lax.all_gather(grad_second, 'tensor', axis=0, tiled=True)  33 us
    reduce_scatter x1, waiting for transfers between devices, local(): lax.psum_scatter(jnp.einsum('tf,df->td', segment, w_in, preferred_element...  31.9 us
    reduce_scatter x2, waiting for transfers between devices, forward_pass(): lax.psum_scatter(jnp.dot(segment, w_down, preferred_element_type=jnp.floa...  31.8 us
  transfers between devices with their start and end apart: 12, of which 9 were waited for; matrix products, arithmetic and copies ran while one was open for 17% of the time, Pallas kernels for 0%

commit v1 on v0

--- a/solution.py
+++ b/solution.py
@@ -1,7 +1,262 @@
+import functools
+
 import jax
 import jax.numpy as jnp
 from jax import lax
+from jax.experimental import pallas as pl
+from jax.experimental.pallas import tpu as pltpu
 from jax.sharding import PartitionSpec as P
+
+MESH = pl.DeviceIdType.MESH
+N_Z, N_X = 4, 2
+TILE = 512
+
+
+def place():
+    dp = lax.axis_index("dp")
+    return dp // (2 * N_X), (dp // 2) % N_X, dp % 2, lax.axis_index("tensor")
+
+
+def at(z, x, c, y):
+    return ((z * N_X + x) * 2 + c, y)
+
+
+def greet(peers):
+    barrier = pltpu.get_barrier_semaphore()
+    for peer in peers:
+        pl.semaphore_signal(barrier, inc=1, device_id=peer, device_id_type=MESH)
+    pl.semaphore_wait(barrier, len(peers))
+
+
+def copy_to(src, dst, send_sem, recv_sem, peer):
+    return pltpu.make_async_remote_copy(
+        src_ref=src, dst_ref=dst, send_sem=send_sem, recv_sem=recv_sem,
+        device_id=peer, device_id_type=MESH,
+    )
+
+
+def gather_kernel(*refs):
+    count = (len(refs) - 2) // 2
+    mine, other = refs[:count], refs[count : 2 * count]
+    send, recv = refs[2 * count :]
+    count = count - 1
+    z, x, c, y = place()
+    zb = z % 2
+    to_y, to_x, to_z, to_c = at(z, x, c, 1 - y), at(z, 1 - x, c, y), at(z + 1 - 2 * zb, x, c, y), at(z, x, 1 - c, y)
+    greet([to_y, to_x, to_z, to_c])
+
+    def rows(n, core, group, first, parts):
+        size = mine[n].shape[0] // 16
+        return pl.ds(pl.multiple_of(core * 8 * size + group * 4 * size + first * size, 8), parts * size)
+
+    def message(n, kind):
+        pair_a, pair_b = (0, 2 * zb, 2), (1, 2 * x, 2)
+        one_a, one_b = (0, 2 * zb + x, 1), (1, 2 * x + zb, 1)
+        far_a, far_b = (0, 2 * (1 - zb), 2), (1, 2 * (1 - x), 2)
+        what, peer = [
+            (one_a, to_y), (one_b, to_y), (one_a, to_x), (one_b, to_z),
+            (pair_a, to_z), (pair_b, to_x), (pair_a, to_c), (pair_b, to_c), (far_a, to_c), (far_b, to_c),
+        ][kind]
+        source = (mine if kind < 2 else other)[n]
+        span = rows(n, c, *what)
+        return copy_to(source.at[span], other[n].at[span], send.at[n, kind], recv.at[n, kind], peer)
+
+    bias = copy_to(mine[count], other[count], send.at[count, 0], recv.at[count, 0], to_y)
+    bias.start()
+    for n in range(count):
+        message(n, 0).start()
+        message(n, 1).start()
+
+    def stage(n, step):
+        if step == 0:
+            message(n, 0).wait_recv(); message(n, 2).start()
+            message(n, 1).wait_recv(); message(n, 3).start()
+        if step == 1:
+            message(n, 2).wait_recv(); message(n, 4).start(); message(n, 6).start()
+            message(n, 3).wait_recv(); message(n, 5).start(); message(n, 7).start()
+        if step == 2:
+            message(n, 4).wait_recv(); message(n, 8).start()
+            message(n, 5).wait_recv(); message(n, 9).start()
+        if step == 3:
+            for kind in (6, 7, 8, 9):
+                message(n, kind).wait_recv()
+            for kind in range(10):
+                message(n, kind).wait_send()
+
+    for t in range(count + 3):
+        for step in range(4):
+            if 0 <= t - step < count:
+                stage(t - step, step)
+    bias.wait()
+
+
+def gather(arrays, collective_id):
+    count = len(arrays)
+    return pl.pallas_call(
+        gather_kernel,
+        out_shape=[jax.ShapeDtypeStruct(a.shape, a.dtype) for a in arrays],
+        in_specs=[pl.BlockSpec(memory_space=pl.ANY)] * count,
+        out_specs=[pl.BlockSpec(memory_space=pl.ANY)] * count,
+        scratch_shapes=[pltpu.SemaphoreType.DMA((count, 10)), pltpu.SemaphoreType.DMA((count, 10))],
+        compiler_params=pltpu.CompilerParams(collective_id=collective_id, has_side_effects=True),
+    )(*arrays)
+
+
+MESSAGES = 12
+
+
+def reduce_kernel(count, own_hbm, oth_hbm, small_in, out_hbm, small_out,
+                  own, oth, r1, ry, rx, rz, agc, stage_buf, small, s0, s1, s2, s3, s4,
+                  load_sem, send, recv, out_sem, small_send, small_recv):
+    z, x, c, y = place()
+    to_c, to_y, to_x = at(z, x, 1 - c, y), at(z, x, c, 1 - y), at(z, 1 - x, c, y)
+    z_of = [(z + d) % N_Z for d in (1, 2, 3)]
+    to_z = [at(v, x, c, y) for v in z_of]
+    for k in range(2):
+        pltpu.make_async_copy(own_hbm.at[pl.ds(k * count // 2, count // 2)], own.at[pl.ds(k * count // 2, count // 2)], load_sem.at[0, k]).start()
+        pltpu.make_async_copy(oth_hbm.at[pl.ds(k * count // 2, count // 2)], oth.at[pl.ds(k * count // 2, count // 2)], load_sem.at[1, k]).start()
+    small[...] = small_in[...]
+    greet([to_c, to_y, to_x] + to_z)
+    half, quarter, part = TILE // 2, TILE // 4, TILE // 16
+    c_rows = pl.ds(pl.multiple_of(c * half, half), half)
+    cn_rows = pl.ds(pl.multiple_of((1 - c) * half, half), half)
+    x_rows = pl.ds(pl.multiple_of(c * half + x * quarter, quarter), quarter)
+    xn_rows = pl.ds(pl.multiple_of(c * half + (1 - x) * quarter, quarter), quarter)
+
+    def z_rows(v):
+        return pl.ds(pl.multiple_of(c * half + x * quarter + v * part, part), part)
+
+    def message(k, kind):
+        if kind == 0: src, dst, peer = own.at[k, cn_rows], r1.at[k, 0], to_c
+        if kind == 1: src, dst, peer = oth.at[k, cn_rows], r1.at[k, 1], to_c
+        if kind == 2: src, dst, peer = oth.at[k, c_rows], ry.at[k], to_y
+        if kind == 3: src, dst, peer = own.at[k, xn_rows], rx.at[k], to_x
+        if 4 <= kind < 7: src, dst, peer = own.at[k, z_rows(z_of[kind - 4])], rz.at[k, kind - 4], to_z[kind - 4]
+        if 7 <= kind < 10: src, dst, peer = oth.at[k, z_rows(z)], oth.at[k, z_rows(z)], to_z[kind - 7]
+        if kind == 10: src, dst, peer = oth.at[k, x_rows], oth.at[k, x_rows], to_x
+        if kind == 11: src, dst, peer = oth.at[k, c_rows], agc.at[k], to_c
+        return copy_to(src, dst, send.at[k, kind], recv.at[k, kind], peer)
+
+    def add_into(dst, src, n):
+        def body(i, _):
+            r = pl.ds(pl.multiple_of(i * 64, 64), 64)
+            dst[r, :] = dst[r, :] + src[r, :]
+            return 0
+        lax.fori_loop(0, n // 64, body, 0)
+
+    def wait(k, kinds):
+        for kind in kinds:
+            message(k, kind).wait()
+
+    def out_copy(k, which):
+        rows = c_rows if which == 0 else cn_rows
+        return pltpu.make_async_copy(stage_buf.at[which, k % 2], out_hbm.at[k, rows], out_sem.at[which, k % 2])
+
+    def widen(k, which):
+        src = oth.at[k, c_rows] if which == 0 else agc.at[k]
+        @pl.when(k >= 2)
+        def _():
+            out_copy(k - 2, which).wait()
+        def body(i, _):
+            r = pl.ds(pl.multiple_of(i * 64, 64), 64)
+            stage_buf[which, k % 2, r, :] = src[r, :].astype(jnp.float32)
+            return 0
+        lax.fori_loop(0, half // 64, body, 0)
+        out_copy(k, which).start()
+
+    def step(k, s):
+        if s == 0:
+            for b in range(2):
+                @pl.when(k == b * count // 2)
+                def _():
+                    pltpu.make_async_copy(own_hbm.at[pl.ds(b * count // 2, count // 2)], own.at[pl.ds(b * count // 2, count // 2)], load_sem.at[0, b]).wait()
+                    pltpu.make_async_copy(oth_hbm.at[pl.ds(b * count // 2, count // 2)], oth.at[pl.ds(b * count // 2, count // 2)], load_sem.at[1, b]).wait()
+            message(k, 0).start(); message(k, 1).start()
+        if s == 1:
+            wait(k, (0, 1))
+            add_into(oth.at[k, c_rows], r1.at[k, 1], half)
+            message(k, 2).start()
+            add_into(own.at[k, c_rows], r1.at[k, 0], half)
+        if s == 2:
+            wait(k, (2,))
+            add_into(own.at[k, c_rows], ry.at[k], half)
+            message(k, 3).start()
+        if s == 3:
+            wait(k, (3,))
+            add_into(own.at[k, x_rows], rx.at[k], quarter)
+            for kind in (4, 5, 6): message(k, kind).start()
+        if s == 4:
+            wait(k, (4, 5, 6))
+            total = own[k, z_rows(z), :].astype(jnp.float32)
+            for d in range(3):
+                total = total + rz[k, d].astype(jnp.float32)
+            oth[k, z_rows(z), :] = total.astype(jnp.bfloat16)
+            for kind in (7, 8, 9): message(k, kind).start()
+        if s == 5:
+            wait(k, (7, 8, 9))
+            message(k, 10).start()
+        if s == 6:
+            wait(k, (10,))
+            message(k, 11).start()
+            widen(k, 0)
+        if s == 7:
+            wait(k, (11,))
+            widen(k, 1)
+
+    zp, zq = at(z + 1 - 2 * (z % 2), x, c, y), at((z + 2) % 4, x, c, y)
+    def small_messages(i):
+        ss, rr = small_send, small_recv
+        if i == 0: return [copy_to(small, s0, ss.at[0], rr.at[0], to_c)]
+        if i == 1: return [copy_to(small.at[pl.ds(0, 8)], s1.at[pl.ds(0, 8)], ss.at[1], rr.at[1], to_y),
+                           copy_to(small.at[pl.ds(16, 8)], s1.at[pl.ds(8, 8)], ss.at[2], rr.at[2], to_y)]
+        if i == 2: return [copy_to(small.at[pl.ds(0, 16)], s2, ss.at[3], rr.at[3], to_x)]
+        if i == 3: return [copy_to(small.at[pl.ds(0, 16)], s3, ss.at[4], rr.at[4], zp)]
+        if i == 4: return [copy_to(small.at[pl.ds(0, 16)], s4, ss.at[5], rr.at[5], zq)]
+    def small_start(i):
+        for m in small_messages(i): m.start()
+    def small_finish(i):
+        for m in small_messages(i): m.wait()
+        if i == 0: small[...] = small[...] + s0[...]
+        else: small[pl.ds(0, 16), :] = small[pl.ds(0, 16), :] + (s1, s2, s3, s4)[i - 1][...]
+
+    def loop(t, _):
+        for s in range(7, -1, -1):
+            @pl.when((t >= s) & (t - s < count))
+            def _():
+                step(t - s, s)
+        for i in range(6):
+            @pl.when(t == i + 1)
+            def _():
+                if i > 0: small_finish(i - 1)
+                if i < 5: small_start(i)
+        return 0
+    lax.fori_loop(0, count + 7, loop, 0)
+    small_out[...] = small[pl.ds(0, 16), :]
+    for k in (count - 2, count - 1):
+        for which in (0, 1):
+            out_copy(k, which).wait()
+
+
+def reduce(own, oth, small, collective_id):
+    count = own.shape[0]
+    h, bf = TILE // 2, jnp.bfloat16
+    V = pltpu.VMEM
+    dma = pltpu.SemaphoreType.DMA
+    any_spec, vm = pl.BlockSpec(memory_space=pl.ANY), pl.BlockSpec(memory_space=pltpu.VMEM)
+    return pl.pallas_call(
+        functools.partial(reduce_kernel, count),
+        out_shape=[jax.ShapeDtypeStruct(own.shape, jnp.float32), jax.ShapeDtypeStruct((16, 1024), jnp.float32)],
+        in_specs=[any_spec, any_spec, vm],
+        out_specs=[any_spec, vm],
+        scratch_shapes=[
+            V((count, TILE, TILE), bf), V((count, TILE, TILE), bf), V((count, 2, h, TILE), bf), V((count, h, TILE), bf),
+            V((count, h // 2, TILE), bf), V((count, 3, h // 8, TILE), bf), V((count, h, TILE), bf),
+            V((2, 2, h, TILE), jnp.float32), V((24, 1024), jnp.float32), V((24, 1024), jnp.float32),
+            V((16, 1024), jnp.float32), V((16, 1024), jnp.float32), V((16, 1024), jnp.float32), V((16, 1024), jnp.float32),
+            dma((2, 2)), dma((count, MESSAGES)), dma((count, MESSAGES)), dma((2, 2)), dma((6,)), dma((6,)),
+        ],
+        compiler_params=pltpu.CompilerParams(collective_id=collective_id, has_side_effects=True, vmem_limit_bytes=60 << 20),
+    )(own, oth, small)
 
 HEAD = 64
 SEQ = 512
@@ -162,7 +417,7 @@
     )
 
 
-def local(
+def general(
     inputs,
     lengths,
     w_qkv,
@@ -297,7 +552,144 @@
     )
 
 
+def split_by_sequence(
+    inputs,
+    lengths,
+    w_qkv,
+    b_qv,
+    w_out,
+    b_out,
+    gain_one,
+    shift_one,
+    w_in,
+    b_in,
+    w_down,
+    b_down,
+    gain_two,
+    shift_two,
+    cotangent,
+):
+    f32, bf = jnp.float32, jnp.bfloat16
+    rows, width = inputs.shape
+    half_width, half_hidden = w_qkv.shape[2], w_in.shape[1]
+    length = lengths[lax.axis_index("tensor")]
+    wq = w_qkv.transpose(1, 0, 2).reshape(3 * width, half_width)
+    bias = jnp.concatenate([b_qv, b_in.reshape(-1, half_width)], axis=0)
+    bias = jnp.pad(bias, ((0, 16 - bias.shape[0]), (0, 0)))
+    own = (wq, w_out, w_in, w_down, bias)
+    halves = [own, gather(list(own), 1)]
+
+    def dot(a, b, ca, cb):
+        return lax.dot_general(a, b, (((ca,), (cb,)), ((), ())), preferred_element_type=f32)
+
+    keys_valid = (jnp.arange(rows) < length)[None, None, :]
+    saved = []
+    branch = b_out.astype(f32)[None]
+    for wq_h, wo_h, wi_h, wd_h, bias_h in halves:
+        w3 = wq_h.reshape(3, width, half_width)
+        q = (dot(inputs, w3[0], 1, 0) + bias_h[0].astype(f32)).astype(bf)
+        k = dot(inputs, w3[1], 1, 0).astype(bf)
+        v = (dot(inputs, w3[2], 1, 0) + bias_h[1].astype(f32)).astype(bf)
+        q, k, v = (t.reshape(rows, -1, HEAD).transpose(1, 0, 2) for t in (q, k, v))
+        s = jnp.einsum("hqe,hke->hqk", q, k, preferred_element_type=f32) * HEAD ** (-0.5)
+        s = jnp.where(keys_valid, s, NEG_FILL)
+        e = jnp.exp(s - jnp.max(s, axis=-1, keepdims=True))
+        p = e / jnp.sum(e, axis=-1, keepdims=True)
+        context = jnp.einsum("hqk,hke->hqe", p.astype(bf), v, preferred_element_type=f32).astype(bf)
+        context = context.transpose(1, 0, 2).reshape(rows, half_width)
+        branch = branch + dot(context, wo_h, 1, 0)
+        saved.append((w3, q, k, v, p, context))
+    normed, xhat1, rstd1 = norm_forward(inputs.astype(f32) + branch, gain_one.astype(f32), shift_one.astype(f32))
+    normed_low = normed.astype(bf)
+    second = b_down.astype(f32)[None]
+    ffn = []
+    for wq_h, wo_h, wi_h, wd_h, bias_h in halves:
+        hidden = dot(normed_low, wi_h, 1, 0) + bias_h[2 : 2 + half_hidden // half_width].reshape(-1).astype(f32)
+        active = gelu_exact(hidden).astype(bf)
+        second = second + dot(active, wd_h, 1, 0)
+        ffn.append((hidden, active))
+    output, xhat2, rstd2 = norm_forward(normed + second, gain_two.astype(f32), shift_two.astype(f32))
+    grad_out = cotangent.astype(f32) * (jnp.arange(rows) < length).astype(f32)[:, None]
+    g_two, g_gain_two, g_shift_two = norm_backward(grad_out, xhat2, rstd2, gain_two.astype(f32))
+    g_second = g_two.astype(bf)
+    g_b_down = jnp.sum(g_second.astype(f32), axis=0)
+    g_normed = g_two
+    tiles = [[], []]
+    smalls = [[], []]
+
+    def tile(n, a):
+        a = a.astype(bf)
+        r, q = a.shape
+        tiles[n].append(a.reshape(r // TILE, TILE, q // TILE, TILE).transpose(0, 2, 1, 3).reshape(-1, TILE, TILE))
+
+    for n, (wq_h, wo_h, wi_h, wd_h, bias_h) in enumerate(halves):
+        hidden, active = ffn[n]
+        tile(n, dot(active, g_second, 0, 0))
+        g_active = dot(g_second, wd_h, 1, 1)
+        g_hidden = jax.vjp(gelu_exact, hidden)[1](g_active)[0].astype(bf)
+        smalls[n].append(jnp.sum(g_hidden.astype(f32), axis=0))
+        tile(n, dot(normed_low, g_hidden, 0, 0))
+        g_normed = g_normed + dot(g_hidden, wi_h, 1, 1)
+    g_first, g_gain_one, g_shift_one = norm_backward(g_normed, xhat1, rstd1, gain_one.astype(f32))
+    g_branch = g_first.astype(bf)
+    g_b_out = jnp.sum(g_branch.astype(f32), axis=0)
+    g_inputs = g_first
+    for n, (wq_h, wo_h, wi_h, wd_h, bias_h) in enumerate(halves):
+        w3, q, k, v, p, context = saved[n]
+        tile(n, dot(context, g_branch, 0, 0))
+        g_context = dot(g_branch, wo_h, 1, 1).astype(bf)
+        gc = g_context.reshape(rows, -1, HEAD).transpose(1, 0, 2)
+        g_p = jnp.einsum("hqe,hke->hqk", gc, v, preferred_element_type=f32)
+        g_v = jnp.einsum("hqk,hqe->hke", p.astype(bf), gc, preferred_element_type=f32)
+        g_s = (p * (g_p - jnp.sum(p * g_p, axis=-1, keepdims=True))).astype(bf)
+        g_q = jnp.einsum("hqk,hke->hqe", g_s, k, preferred_element_type=f32) * HEAD ** (-0.5)
+        g_k = jnp.einsum("hqk,hqe->hke", g_s, q, preferred_element_type=f32) * HEAD ** (-0.5)
+        for i, g in enumerate((g_q, g_k, g_v)):
+            g = g.transpose(1, 0, 2).reshape(rows, half_width).astype(bf)
+            tile(n, dot(inputs, g, 0, 0))
+            g_inputs = g_inputs + dot(g, w3[i], 1, 1)
+            if i != 1:
+                smalls[n].append(jnp.sum(g.astype(f32), axis=0))
+    shared = jnp.stack([g_gain_one, g_shift_one, g_b_out, g_gain_two, g_shift_two, g_b_down])
+    pad = lambda a: jnp.pad(a, ((0, 8 - a.shape[0]), (0, 0)))
+    pieces = [pad(jnp.concatenate([s.reshape(-1) for s in smalls[n]]).reshape(-1, width)) for n in (0, 1)]
+    small = jnp.concatenate([pad(shared), pieces[0], pieces[1]], axis=0)
+    sums, small_sums = reduce(jnp.concatenate(tiles[0]), jnp.concatenate(tiles[1]), small, 2)
+
+    def untile(first, r, q):
+        count = (r // TILE) * (q // TILE)
+        a = sums[first : first + count].reshape(r // TILE, q // TILE, TILE, TILE)
+        return a.transpose(0, 2, 1, 3).reshape(r, q), first + count
+
+    at_tile = 0
+    g_w_down, at_tile = untile(at_tile, half_hidden, width)
+    g_w_in, at_tile = untile(at_tile, width, half_hidden)
+    g_w_out, at_tile = untile(at_tile, half_width, width)
+    g_w_qkv, at_tile = untile(at_tile, 3 * width, half_width)
+    owned = small_sums[8:].reshape(-1)
+    g_b_in = owned[:half_hidden]
+    g_b_qv = owned[half_hidden : half_hidden + 2 * half_width].reshape(2, half_width)
+    return (
+        output.astype(bf),
+        g_inputs.astype(bf),
+        g_w_qkv.reshape(3, width, half_width).transpose(1, 0, 2),
+        g_b_qv,
+        g_w_out,
+        small_sums[2],
+        small_sums[0],
+        small_sums[1],
+        g_w_in,
+        g_b_in,
+        g_w_down,
+        small_sums[5],
+        small_sums[3],
+        small_sums[4],
+    )
+
+
 def solution(mesh):
+    small_mesh = mesh.shape["tensor"] == 2 and mesh.shape["dp"] == 4 * N_Z
+    step = split_by_sequence if small_mesh else general
     in_specs = (
         P(("dp", "tensor"), None),
         P("dp"),
@@ -331,4 +723,4 @@
         P(),
         P(),
     )
-    return jax.shard_map(local, mesh=mesh, in_specs=in_specs, out_specs=out_specs, check_vma=False)
+    return jax.shard_map(step, mesh=mesh, in_specs=in_specs, out_specs=out_specs, check_vma=False)

time: 831 us -> 648 us (0.78)
  waiting for transfers between devices: 416 us -> 0 us
  Pallas kernels: 0 us -> 274 us
  local copies, waits for them, and re-layouts: 63.9 us -> 167 us
  blocking collectives: 71.2 us -> 0 us
  other arithmetic: 68.3 us -> 20.9 us
  between operations: 15.3 us -> 1.52 us
    pallas_call x0 -> x2, Pallas kernels: none -> 274 us  [the longest x1 202 us: reduce(): pl.pallas_call(functools.partial(reduce_kernel, count), out_shape=[jax.Sh...]
    psum x1 -> x0, waiting for transfers between devices: 165 us -> none  [local(): lax.psum(grad_w_qkv.astype(jnp.bfloat16), 'dp').astype(jnp.float32)]
    all_gather x5 -> x0, waiting for transfers between devices: 156 us -> none  [the longest x2 56.5 us: forward_pass(): lax.all_gather(normed.astype(jnp.bfloat16), 'tensor', axis=0, tiled=True)]
    reduce_scatter x6 -> x0, waiting for transfers between devices: 93.6 us -> none  [the longest x1 31.9 us: local(): lax.psum_scatter(jnp.einsum('tf,df->td', segment, w_in, preferred_element...]
    psum x2 -> x0, blocking collectives: 71.2 us -> none  [the longest x1 63.7 us: local(): lax.psum(small_terms.astype(jnp.bfloat16), 'dp').astype(jnp.float32)]
    reshape x3 -> x14, local copies, waits for them, and re-layouts: 16.1 us -> 56.3 us  [the longest x10 55 us: tile(): a.reshape(r // TILE, TILE, q // TILE, TILE).transpose(0, 2, 1, 3)]
    unnamed x105 -> x138, local copies, waits for them, and re-layouts: 12.2 us -> 42.8 us
    transpose x0 -> x4, local copies, waits for them, and re-layouts: none -> 29.4 us  [untile(): return (a.transpose(0, 2, 1, 3).reshape(r, q), first + count)]
  transfers between devices with their start and end apart: 12 -> 0, of which waited for: 9 -> 0; matrix products, arithmetic and copies ran while one was open for 17% -> 0% of each run, Pallas kernels for 0% -> 0%
where the time goes in v1:
time: 648 us; the launch traced here: 643 us
  Pallas kernels  274 us (42%)
  matrix products  179 us (28%)
  local copies, waits for them, and re-layouts  167 us (26%)
  other arithmetic  20.9 us (3%)
    pallas_call x1, Pallas kernels, reduce(): pl.pallas_call(functools.partial(reduce_kernel, count), out_shape=[jax.Sh...  202 us
    dot_general x36, matrix products, dot(): lax.dot_general(a, b, (((ca,), (cb,)), ((), ())), preferred_element_type=...  129 us
    pallas_call x1, Pallas kernels, gather(): pl.pallas_call(gather_kernel, out_shape=[jax.ShapeDtypeStruct(a.shape, a....  72.6 us
    reshape x10, local copies, waits for them, and re-layouts, tile(): a.reshape(r // TILE, TILE, q // TILE, TILE).transpose(0, 2, 1, 3)  55 us
    unnamed x138, local copies, waits for them, and re-layouts  42.8 us
    transpose x4, local copies, waits for them, and re-layouts, untile(): return (a.transpose(0, 2, 1, 3).reshape(r, q), first + count)  29.4 us
    slice x2, local copies, waits for them, and re-layouts, untile(): a = sums[first:first + count].reshape(r // TILE, q // TILE, TILE, TILE)  16.5 us
    convert_element_type x8, local copies, waits for them, and re-layouts, tile(): a = a.astype(bf)  16.4 us

profile of v1, /device:TPU:0, one launch (start us, length us, event | category | flops | bytes accessed | tf_op | source)
XLA Modules:
  0.0 643.1 jit_solution(11058613310593822809)
XLA Ops:
  17.8 5.8 fusion.90
  29.6 72.6 %shard_map.254 = (bf16[3072,512]{1,0:T(8,128)(2,1)}, bf16[512,1024]{1,0:T(8,128)(2,1)}, bf16[1024,2048]{1,0:T(8,128)(2,1)}, bf16[2048,1024]{1,0:T(8,128)(2,1)}, bf16[16,512]{1,0:T(8,128)(2,1)}) custom-call(bf16[3072,512]{1,0:T(8,128)(2,1)} %bitcast.251, bf16[512,1024]{1,0:T(8,128)(2,1)} %refs_1_.1, bf16[1024,2048]{1,0:T(8,128)(2,1)} %refs_2_.1, ...), custom_call_target="tpu_custom_call" | custom-call | tf_op jit(solution)/shard_map/pallas_call | solution.py:95
  112.1 7.9 %fusion.91 = (f32[8,512]{1,0:T(8,128)S(1)}, f32[8,512,512]{1,2,0:T(8,128)}) fusion(pred[512]{0:T(512)(128)(4,1)S(1)} %get-tuple-element.100, bf16[8,512,64]{1,2,0:T(8,128)(2,1)} %bitcast.285, bf16[8,512,64]{1,2,0:T(8,128)(2,1)} %bitcast.283), kind=kOutput, calls=%fused_computation.202 | convolution fusion | flops 276824576 | bytes 9454080 | tf_op jit(solution)/shard_map/sub | solution.py:596
  127.6 12.8 %multiply_convert_fusion.2 = (bf16[512,2048]{1,0:T(8,128)(2,1)S(1)}, f32[512,2048]{1,0:T(8,128)}, f32[512,2048]{1,0:T(8,128)}) fusion(f32[2048]{0:T(1024)S(1)} %bitcast.299, bf16[512,1024]{1,0:T(8,128)(2,1)S(1)} %fusion.33, bf16[1024,2048]{1,0:T(8,128)(2,1)S(1)} %copy-done.41), kind=kOutput, calls=%fused_computation.20 | convolution fusion | flops 2216689664 | bytes 15736832 | tf_op jit(solution)/shard_map/dot_general | solution.py:583
  140.4 12.7 %multiply_convert_fusion.3 = (bf16[512,2048]{1,0:T(8,128)(2,1)S(1)}, f32[512,2048]{1,0:T(8,128)}, f32[512,2048]{1,0:T(8,128)}) fusion(f32[2048]{0:T(1024)S(1)} %convert_element_type.322, bf16[512,1024]{1,0:T(8,128)(2,1)S(1)} %fusion.33, bf16[1024,2048]{1,0:T(8,128)(2,1)S(1)} %copy-done.11), kind=kOutput, calls=%fused_computation.33 | convolution fusion | flops 2216689664 | bytes 15736832 | tf_op jit(solution)/shard_map/dot_general | solution.py:583
  162.0 6.5 %convert_reduce_fusion = (f32[2048]{0:T(1024)S(1)}, bf16[512,2048]{1,0:T(8,128)(2,1)S(1)}) fusion(f32[512,2048]{1,0:T(8,128)} %get-tuple-element.60, f32[512,2048]{1,0:T(8,128)} %get-tuple-element.84, f32[2048]{0:T(1024)S(1)} %bitcast.300, bf16[512,1024]{1,0:T(8,128)(2,1)S(1)} %get-tuple-element.51, bf16[2048,1024]{1,0:T(8,128)(2,1)S(1)} %copy-done.42), kind=kOutput, calls=%fused_computation.16 | convolution fusion | flops 2165307392 | bytes 15745024 | tf_op jit(solution)/shard_map/dot_general | solution.py:583
  168.6 6.9 %convert_reduce_fusion.1 = (f32[2048]{0:T(1024)S(1)}, bf16[512,2048]{1,0:T(8,128)(2,1)S(1)}) fusion(f32[512,2048]{1,0:T(8,128)} %get-tuple-element.62, f32[512,2048]{1,0:T(8,128)} %get-tuple-element.83, f32[2048]{0:T(1024)S(1)} %convert_element_type.322, bf16[512,1024]{1,0:T(8,128)(2,1)S(1)} %get-tuple-element.51, bf16[2048,1024]{1,0:T(8,128)(2,1)S(1)} %copy-done.10), kind=kOutput, calls=%fused_computation.17 | convolution fusion | flops 2165307392 | bytes 15745024 | tf_op jit(solution)/shard_map/dot_general | solution.py:583
  195.1 5.6 convert_reduce_fusion.6
  219.2 6.3 convolution_convert_fusion
  225.5 7.9 %reshape.251 = bf16[2,512,4,512]{3,2,1,0:T(4,128)(2,1)} reshape(bf16[1024,2048]{1,0:T(8,128)(2,1)} %convolution_convert_fusion) | data formatting | bytes 8388608 | tf_op jit(solution)/shard_map/reshape | solution.py:623
  233.4 5.2 copy.65
  243.0 8.0 %reshape.245 = bf16[2,512,4,512]{3,2,1,0:T(4,128)(2,1)} reshape(bf16[1024,2048]{1,0:T(8,128)(2,1)} %convolution_convert_fusion.2) | data formatting | bytes 8388608 | tf_op jit(solution)/shard_map/reshape | solution.py:623
  251.0 5.2 copy.58
  260.6 7.8 %reshape.249 = bf16[4,512,2,512]{3,2,1,0:T(2,128)(2,1)} reshape(bf16[2048,1024]{1,0:T(8,128)(2,1)} %convolution_convert_fusion.1) | data formatting | bytes 8388608 | tf_op jit(solution)/shard_map/reshape | solution.py:623
  268.5 5.1 copy.64
  278.0 7.8 %reshape.243 = bf16[4,512,2,512]{3,2,1,0:T(2,128)(2,1)} reshape(bf16[2048,1024]{1,0:T(8,128)(2,1)} %convolution_convert_fusion.3) | data formatting | bytes 8388608 | tf_op jit(solution)/shard_map/reshape | solution.py:623
  285.8 5.0 copy.57
  373.5 201.8 %shard_map.255 = (f32[24,512,512]{2,1,0:T(8,128)}, f32[16,1024]{1,0:T(8,128)}) custom-call(bf16[24,512,512]{2,1,0:T(8,128)(2,1)} %constant_dynamic-update-slice_fusion.own_hbm, bf16[24,512,512]{2,1,0:T(8,128)(2,1)} %constant_dynamic-update-slice_fusion.5.oth_hbm, f32[24,1024]{1,0:T(8,128)} %select_maximum_fusion.small_in), custom_call_target="tpu_custom_call" | custom-call | tf_op jit(solution)/shard_map/pallas_call | solution.py:246
  585.7 6.9 %slice.102 = f32[6,512,512]{2,1,0:T(8,128)} slice(f32[24,512,512]{2,1,0:T(8,128)} %get-tuple-element.26), slice={[18:24], [0:512], [0:512]} | slice | bytes 12582912 | tf_op jit(solution)/shard_map/slice | solution.py:661
  592.6 9.6 %fusion.88 = (f32[8,512,512]{2,1,0:T(8,128)S(1)}, f32[8,512,512]{2,1,0:T(8,128)}) fusion(f32[24,512,512]{2,1,0:T(8,128)} %get-tuple-element.26), kind=kLoop, calls=%fused_computation.199 | loop fusion | bytes 33554432 | tf_op jit(solution)/shard_map/slice | solution.py:661
  602.2 12.4 %copy.73 = f32[4,512,2,512]{3,2,1,0:T(2,128)S(1)} copy(f32[4,512,2,512]{3,1,2,0:T(8,128)S(1)} %bitcast.243) | data formatting | bytes 16777216 | tf_op jit(solution)/shard_map/transpose | solution.py:662
  614.6 5.5 copy.86
  620.1 12.0 %copy.72 = f32[2,512,4,512]{3,2,1,0:T(4,128)} copy(f32[2,512,4,512]{3,1,2,0:T(8,128)} %bitcast.242) | data formatting | bytes 16777216 | tf_op jit(solution)/shard_map/transpose | solution.py:662
  632.1 10.9 %copy.84 = f32[128,8,4,512]{3,1,2,0:T(8,128)} copy(f32[128,8,4,512]{3,2,1,0:T(4,128)} %bitcast.241) | data formatting | bytes 16777216
  (234 shorter events, 193.3 us)
Async XLA Ops:
  0.6 15.0 %copy-start.23 = (bf16[512,1024]{1,0:T(8,128)(2,1)S(1)}, bf16[512,1024]{1,0:T(8,128)(2,1)}, u32[]{:S(2)}) copy-start(bf16[512,1024]{1,0:T(8,128)(2,1)} %param.15) | copy-start | bytes 3145732
  15.6 8.0 %copy-start.32 = (bf16[512,512]{0,1:T(8,128)(2,1)}, bf16[512,512]{0,1:T(8,128)(2,1)S(1)}, u32[]{:S(2)}) copy-start(bf16[512,512]{0,1:T(8,128)(2,1)S(1)} %fusion.40) | copy-start | bytes 1572868
  17.8 5.8 copy-start.30
  17.8 5.8 copy-start.43
  23.6 5.2 copy-start.8
  29.6 74.1 %copy-start.24 = (bf16[512,1024]{1,0:T(8,128)(2,1)S(1)}, bf16[512,1024]{1,0:T(8,128)(2,1)}, u32[]{:S(2)}) copy-start(bf16[512,1024]{1,0:T(8,128)(2,1)} %param.15) | copy-start | bytes 3145732
  127.6 12.8 %copy-start.21 = (bf16[512,1024]{1,0:T(8,128)(2,1)}, bf16[512,1024]{1,0:T(8,128)(2,1)S(1)}, u32[]{:S(2)}) copy-start(bf16[512,1024]{1,0:T(8,128)(2,1)S(1)} %fusion.33) | copy-start | bytes 3145732
  127.6 12.8 %copy-start.11 = (bf16[1024,2048]{1,0:T(8,128)(2,1)S(1)}, bf16[1024,2048]{1,0:T(8,128)(2,1)}, u32[]{:S(2)}) copy-start(bf16[1024,2048]{1,0:T(8,128)(2,1)} %refs_2_.1) | copy-start | bytes 12582916
  140.4 15.1 %copy-start.55 = (bf16[512,2048]{1,0:T(8,128)(2,1)}, bf16[512,2048]{1,0:T(8,128)(2,1)S(1)}, u32[]{:S(2)}) copy-start(bf16[512,2048]{1,0:T(8,128)(2,1)S(1)} %get-tuple-element.59) | copy-start | bytes 6291460
  140.4 12.7 %copy-start.10 = (bf16[2048,1024]{1,0:T(8,128)(2,1)S(1)}, bf16[2048,1024]{1,0:T(8,128)(2,1)}, u32[]{:S(2)}) copy-start(bf16[2048,1024]{1,0:T(8,128)(2,1)} %refs_3_.1) | copy-start | bytes 12582916
  162.0 6.5 %copy-start.27 = (bf16[512,1024]{1,0:T(8,128)(2,1)}, bf16[512,1024]{1,0:T(8,128)(2,1)S(1)}, u32[]{:S(2)}) copy-start(bf16[512,1024]{1,0:T(8,128)(2,1)S(1)} %get-tuple-element.51) | copy-start | bytes 3145732
  168.6 9.3 %copy-start.50 = (bf16[512,2048]{1,0:T(8,128)(2,1)}, bf16[512,2048]{1,0:T(8,128)(2,1)S(1)}, u32[]{:S(2)}) copy-start(bf16[512,2048]{1,0:T(8,128)(2,1)S(1)} %get-tuple-element.58) | copy-start | bytes 6291460
  195.1 5.7 copy-start.48
  200.7 5.8 copy-start.25
  208.2 7.8 %copy-start.4 = (bf16[1024,3,512]{2,0,1:T(8,128)(2,1)S(1)}, bf16[1024,3,512]{2,0,1:T(8,128)(2,1)}, u32[]{:S(2)}) copy-start(bf16[1024,3,512]{2,0,1:T(8,128)(2,1)} %param.17) | copy-start | bytes 9437188
  233.4 5.2 copy-start.22
  233.4 5.2 copy-start.52
  251.0 5.2 copy-start.28
  251.0 5.2 copy-start.56
  268.5 5.1 copy-start.54
  290.9 5.8 slice-start.3
  314.0 7.2 %copy-start.44 = (bf16[512,512]{0,1:T(8,128)(2,1)S(1)}, bf16[512,512]{0,1:T(8,128)(2,1)}, u32[]{:S(2)}) copy-start(bf16[512,512]{0,1:T(8,128)(2,1)} %fusion.41) | copy-start | bytes 1572868
  314.0 7.2 %copy-start.47 = (bf16[512,512]{0,1:T(8,128)(2,1)S(1)}, bf16[512,512]{0,1:T(8,128)(2,1)}, u32[]{:S(2)}) copy-start(bf16[512,512]{0,1:T(8,128)(2,1)} %convolution_convert_fusion.13) | copy-start | bytes 1572868
  317.6 8.5 %slice-start = ((s8[8388608]{0:T(1024)(128)(4,1)}), s8[4194304]{0:T(1024)(128)(4,1)S(1)}, s32[]{:S(2)}) async-start(s8[8388608]{0:T(1024)(128)(4,1)} %bitcast.255), calls=%async_computation | async-start | bytes 8388608
  (37 other events, 122.4 us)

commit v2 on v0

--- a/solution.py
+++ b/solution.py
@@ -1,7 +1,15 @@
 import jax
 import jax.numpy as jnp
 from jax import lax
+from jax.experimental import pallas as pl
+from jax.experimental.pallas import tpu as pltpu
 from jax.sharding import PartitionSpec as P
+
+MESH = pl.DeviceIdType.MESH
+N_Z, N_X = 4, 2
+TILE = 512
+MESSAGES = 12
+VMEM_BYTES = 63 << 20
 
 HEAD = 64
 SEQ = 512
@@ -162,7 +170,7 @@
     )
 
 
-def local(
+def general(
     inputs,
     lengths,
     w_qkv,
@@ -297,7 +305,647 @@
     )
 
 
+def place():
+    dp = lax.axis_index("dp")
+    return dp // (2 * N_X), (dp // 2) % N_X, dp % 2, lax.axis_index("tensor")
+
+
+def at(z, x, c, y):
+    return ((z * N_X + x) * 2 + c, y)
+
+
+def greet(peers):
+    barrier = pltpu.get_barrier_semaphore()
+    for peer in peers:
+        pl.semaphore_signal(barrier, inc=1, device_id=peer, device_id_type=MESH)
+    pl.semaphore_wait(barrier, len(peers))
+
+
+def copy_to(src, dst, send_sem, recv_sem, peer):
+    return pltpu.make_async_remote_copy(
+        src_ref=src, dst_ref=dst, send_sem=send_sem, recv_sem=recv_sem,
+        device_id=peer, device_id_type=MESH,
+    )
+
+
+CHUNKS = 24
+RING = 4
+BF, F32 = jnp.bfloat16, jnp.float32
+ROWS_AT_ONCE = 32
+
+
+def dot(a, b, ca, cb):
+    return lax.dot_general(a, b, (((ca,), (cb,)), ((), ())), preferred_element_type=F32)
+
+
+def span(index, size):
+    return pl.ds(pl.multiple_of(index * size, size), size)
+
+
+def layer_kernel(
+    lengths, x_hbm, cot_hbm, wq_own, wo_own, wi_own, wd_own, vec, bias_own,
+    out_hbm, gin_hbm, tiles_hbm, small_out, wq_oth, wo_oth, wi_oth, wd_oth, e_hbm,
+    xv, nlow, gsec, gctx, ctx, qkv, inv, xhat, rs1, acc, u1, u2, own, oth, r1, ry, rx, rz,
+    ring_a, ring_b, bias_oth, small, s0, s1, s2, s3, s4,
+    load_sem, a_sem, b_sem, e_sem, o_sem, t_sem, g_send, g_recv, send, recv, small_send, small_recv,
+):
+    z, x, c, y = place()
+    zb = z % 2
+    z_of = [(z + d) % N_Z for d in (1, 2, 3)]
+    to_c, to_y, to_x = at(z, x, 1 - c, y), at(z, x, c, 1 - y), at(z, 1 - x, c, y)
+    to_z = [at(v, x, c, y) for v in z_of]
+    to_zp, to_zq = at(z + 1 - 2 * zb, x, c, y), at((z + 2) % N_Z, x, c, y)
+    seq, width = xv.shape
+    half_w = width // 2
+
+    load_x = pltpu.make_async_copy(x_hbm, xv, load_sem.at[0])
+    load_cot = pltpu.make_async_copy(cot_hbm, gsec, load_sem.at[1])
+    load_x.start()
+    load_cot.start()
+
+    def fetch_qkv(h, i):
+        source = (wq_own, wq_oth)[h]
+        return pltpu.make_async_copy(source.at[i], ring_b.at[i], b_sem.at[i])
+
+    def fetch_out(h):
+        return pltpu.make_async_copy((wo_own, wo_oth)[h], ring_a.at[h], a_sem.at[h])
+
+    def fetch_in(h, f, slot):
+        return pltpu.make_async_copy((wi_own, wi_oth)[h].at[:, span(f, TILE)], ring_b.at[slot], b_sem.at[slot])
+
+    def fetch_down(h, f, slot):
+        return pltpu.make_async_copy((wd_own, wd_oth)[h].at[span(f, TILE)], ring_a.at[slot], a_sem.at[slot])
+
+    for i in range(3):
+        fetch_qkv(0, i).start()
+    fetch_out(0).start()
+
+    greet([to_c, to_y, to_x] + to_z)
+
+    cut = wi_own.shape[1] // 2
+    deep = wd_own.shape[0] // 2
+    arrays = [(wq_own.at[i], wq_oth.at[i]) for i in range(3)] + [(wo_own, wo_oth)]
+    for j in range(2):
+        arrays.append((wi_own.at[:, j * cut : (j + 1) * cut], wi_oth.at[:, j * cut : (j + 1) * cut]))
+        arrays.append((wd_own.at[j * deep : (j + 1) * deep], wd_oth.at[j * deep : (j + 1) * deep]))
+    count = len(arrays)
+
+    def gather_message(n, kind):
+        size = arrays[n][0].shape[0] // 16
+        pair_a, pair_b = (0, 2 * zb, 2), (1, 2 * x, 2)
+        one_a, one_b = (0, 2 * zb + x, 1), (1, 2 * x + zb, 1)
+        far_a, far_b = (0, 2 * (1 - zb), 2), (1, 2 * (1 - x), 2)
+        (group, first, parts), peer = [
+            (one_a, to_y), (one_b, to_y), (one_a, to_x), (one_b, to_zp),
+            (pair_a, to_zp), (pair_b, to_x), (pair_a, to_c), (pair_b, to_c), (far_a, to_c), (far_b, to_c),
+        ][kind]
+        rows = pl.ds(pl.multiple_of(c * 8 * size + group * 4 * size + first * size, 16), parts * size)
+        source = arrays[n][0 if kind < 2 else 1]
+        return copy_to(source.at[rows], arrays[n][1].at[rows], g_send.at[n, kind], g_recv.at[n, kind], peer)
+
+    def gather_stage(n, step):
+        if step == 0:
+            gather_message(n, 0).wait_recv()
+            gather_message(n, 2).start()
+            gather_message(n, 1).wait_recv()
+            gather_message(n, 3).start()
+        if step == 1:
+            gather_message(n, 2).wait_recv()
+            gather_message(n, 4).start()
+            gather_message(n, 6).start()
+            gather_message(n, 3).wait_recv()
+            gather_message(n, 5).start()
+            gather_message(n, 7).start()
+        if step == 2:
+            gather_message(n, 4).wait_recv()
+            gather_message(n, 8).start()
+            gather_message(n, 5).wait_recv()
+            gather_message(n, 9).start()
+        if step == 3:
+            for kind in (6, 7, 8, 9):
+                gather_message(n, kind).wait_recv()
+            for kind in range(10):
+                gather_message(n, kind).wait_send()
+
+    def progress(slot):
+        for step in range(4):
+            if 0 <= slot - step < count:
+                gather_stage(slot - step, step)
+
+    send_bias = copy_to(bias_own, bias_oth, g_send.at[count, 0], g_recv.at[count, 0], to_y)
+    send_bias.start()
+    for n in range(count):
+        gather_message(n, 0).start()
+        gather_message(n, 1).start()
+
+    length = lengths[y]
+    key_fill = jnp.where(lax.broadcasted_iota(jnp.int32, (1, seq), 1) < length, 0.0, NEG_FILL)
+    low_lanes = lax.broadcasted_iota(jnp.int32, (1, 128), 1) < HEAD
+    one, zero = jnp.ones((), BF), jnp.zeros((), BF)
+    scale = HEAD ** (-0.5)
+    pairs = half_w // 128
+
+    def project(h):
+        bias = (bias_own, bias_oth)[h]
+        for i in range(3):
+            fetch_qkv(h, i).wait()
+            value = dot(xv[...], ring_b[i], 1, 0)
+            if i == 0:
+                qkv[h, 0] = (value + bias[0:1, :]).astype(BF) * jnp.asarray(scale, BF)
+            if i == 1:
+                qkv[h, 1] = value.astype(BF)
+            if i == 2:
+                qkv[h, 2] = (value + bias[1:2, :]).astype(BF)
+
+    def attend(h, p, e_ref):
+        lanes = span(p, 128)
+        q2, k2, v2 = qkv[h, 0, :, lanes], qkv[h, 1, :, lanes], qkv[h, 2, :, lanes]
+        parts = []
+        for head in range(2):
+            mine = low_lanes if head == 0 else jnp.logical_not(low_lanes)
+            scores = dot(jnp.where(mine, q2, zero), k2, 1, 1) + key_fill
+            peak = jnp.max(scores, axis=-1, keepdims=True)
+            e = jnp.exp(scores - peak).astype(BF)
+            e_ref[2 * p + head] = e
+            parts.append(dot(e, jnp.where(mine, v2, one), 1, 0))
+        total = pltpu.roll(jnp.where(low_lanes, parts[1], parts[0]), HEAD, 1)
+        inverse = 1.0 / total
+        inv[h, :, lanes] = inverse
+        ctx[:, span(h * pairs + p, 128)] = (jnp.where(low_lanes, parts[0], parts[1]) * inverse).astype(BF)
+
+    def attend_half(h, slots):
+        def body(p, _):
+            attend(h, p, (u1, u2)[h])
+            for at_pair, slot in slots:
+                @pl.when(p == at_pair)
+                def _():
+                    progress(slot)
+            return 0
+        lax.fori_loop(0, pairs, body, 0)
+
+    def e_copy(h, back):
+        ref, buf = e_hbm.at[pl.ds(h * 8, 8)], (u1 if back else (u1, u2)[h])
+        return pltpu.make_async_copy(ref, buf, e_sem.at[h]) if back else pltpu.make_async_copy(buf, ref, e_sem.at[h])
+
+    load_x.wait()
+    project(0)
+    attend_half(0, ((1, 0), (3, 1)))
+    e_copy(0, False).start()
+    fetch_out(0).wait()
+    acc[...] = dot(ctx[:, :half_w], ring_a[0], 1, 0)
+    for slot in (2, 3):
+        progress(slot)
+    send_bias.wait()
+    fetch_qkv(1, 0).start()
+    progress(4)
+    fetch_qkv(1, 1).start()
+    progress(5)
+    fetch_qkv(1, 2).start()
+    project(1)
+    attend_half(1, ((2, 6),))
+    e_copy(1, False).start()
+    fetch_out(1).start()
+    for f in range(2):
+        fetch_in(0, f, f).start()
+    fetch_down(0, 0, 0).start()
+    fetch_out(1).wait()
+    acc[...] += dot(ctx[:, half_w:], ring_a[1], 1, 0)
+    progress(7)
+
+    def blocks(body):
+        def run(b, _):
+            body(span(b, ROWS_AT_ONCE), b)
+            return 0
+        lax.fori_loop(0, seq // ROWS_AT_ONCE, run, 0)
+
+    def mean(v):
+        return jnp.sum(v, axis=-1, keepdims=True) * (1.0 / width)
+
+    small[...] = jnp.zeros_like(small)
+    b_out, gain1, shift1 = vec[0:1, :], vec[1:2, :], vec[2:3, :]
+    b_down, gain2, shift2 = vec[3:4, :], vec[4:5, :], vec[5:6, :]
+
+    def norm_one(r, b):
+        v = xv[r, :].astype(F32) + (acc[r, :] + b_out)
+        center = v - mean(v)
+        inverse = lax.rsqrt(mean(center * center) + EPSILON)
+        hat = center * inverse
+        xhat[r, :] = hat
+        rs1[r, :] = jnp.broadcast_to(inverse, (ROWS_AT_ONCE, 128))
+        nlow[r, :] = (hat * gain1 + shift1).astype(BF)
+    blocks(norm_one)
+    acc[...] = jnp.zeros_like(acc)
+    e_copy(0, False).wait()
+    e_copy(1, False).wait()
+
+    def hidden_half(h, slots):
+        bias = (bias_own, bias_oth)[h]
+        def body(f, _):
+            t = h * 4 + f
+            b_slot, a_slot = t % 3, t % 2
+            @pl.when(f + 2 < 4)
+            def _():
+                fetch_in(h, f + 2, (t + 2) % 3).start()
+            @pl.when(f + 1 < 4)
+            def _():
+                fetch_down(h, f + 1, (t + 1) % 2).start()
+            fetch_in(h, f, b_slot).wait()
+            hidden = dot(nlow[...], ring_b[b_slot], 1, 0) + bias[pl.ds(2 + f, 1), :]
+            cdf = 0.5 + 0.5 * lax.erf(hidden * 0.7071067811865476)
+            u1[t] = (hidden * cdf).astype(BF)
+            u2[t] = (cdf + hidden * (jnp.exp(hidden * hidden * -0.5) * 0.3989422804014327)).astype(BF)
+            fetch_down(h, f, a_slot).wait()
+            acc[...] += dot(u1[t], ring_a[a_slot], 1, 0)
+            for at_tile, slot in slots:
+                @pl.when(f == at_tile)
+                def _():
+                    progress(slot)
+            return 0
+        lax.fori_loop(0, 4, body, 0)
+
+    hidden_half(0, ((0, 8), (2, 9)))
+    for g in range(2):
+        fetch_in(1, g, (4 + g) % 3).start()
+    fetch_down(1, 0, 0).start()
+    hidden_half(1, ((0, 10),))
+
+    load_cot.wait()
+    valid_limit = lengths[y]
+
+    def norm_two(r, b):
+        normed = xhat[r, :] * gain1 + shift1
+        v = normed + (acc[r, :] + b_down)
+        center = v - mean(v)
+        inverse = lax.rsqrt(mean(center * center) + EPSILON)
+        hat = center * inverse
+        gctx[r, :] = (hat * gain2 + shift2).astype(BF)
+        position = b * ROWS_AT_ONCE + lax.broadcasted_iota(jnp.int32, (ROWS_AT_ONCE, 1), 0)
+        g_out = jnp.where(position < valid_limit, gsec[r, :].astype(F32), 0.0)
+        scaled = g_out * gain2
+        g_two = inverse * (scaled - mean(scaled) - hat * mean(scaled * hat))
+        low = g_two.astype(BF)
+        acc[r, :] = g_two
+        gsec[r, :] = low
+        small[3:4, :] += jnp.sum(g_out * hat, axis=0, keepdims=True)
+        small[4:5, :] += jnp.sum(g_out, axis=0, keepdims=True)
+        small[5:6, :] += jnp.sum(low.astype(F32), axis=0, keepdims=True)
+    blocks(norm_two)
+    out_copy = pltpu.make_async_copy(gctx, out_hbm, o_sem.at[0])
+    gin_copy = pltpu.make_async_copy(nlow, gin_hbm, o_sem.at[1])
+    out_copy.start()
+
+    half, quarter, part = TILE // 2, TILE // 4, TILE // 16
+    c_rows = span(c, half)
+    cn_rows = span(1 - c, half)
+    x_rows = pl.ds(pl.multiple_of(c * half + x * quarter, quarter), quarter)
+    xn_rows = pl.ds(pl.multiple_of(c * half + (1 - x) * quarter, quarter), quarter)
+
+    def z_rows(v):
+        return pl.ds(pl.multiple_of(c * half + x * quarter + v * part, part), part)
+
+    def message(k, kind):
+        slot = k % RING
+        if kind == 0: src, dst, peer = own.at[k, cn_rows], r1.at[slot, 0], to_c
+        if kind == 1: src, dst, peer = oth.at[k, cn_rows], r1.at[slot, 1], to_c
+        if kind == 2: src, dst, peer = oth.at[k, c_rows], ry.at[slot], to_y
+        if kind == 3: src, dst, peer = own.at[k, xn_rows], rx.at[slot], to_x
+        if 4 <= kind < 7: src, dst, peer = own.at[k, z_rows(z_of[kind - 4])], rz.at[slot, kind - 4], to_z[kind - 4]
+        if 7 <= kind < 10: src, dst, peer = oth.at[k, z_rows(z)], oth.at[k, z_rows(z)], to_z[kind - 7]
+        if kind == 10: src, dst, peer = oth.at[k, x_rows], oth.at[k, x_rows], to_x
+        if kind == 11: src, dst, peer = oth.at[k, c_rows], tiles_hbm.at[k, c_rows], to_c
+        return copy_to(src, dst, send.at[slot, kind], recv.at[slot, kind], peer)
+
+    def tile_copy(k):
+        return pltpu.make_async_copy(oth.at[k, c_rows], tiles_hbm.at[k, c_rows], t_sem.at[k % RING])
+
+    def add_into(dst, src, n):
+        def body(i, _):
+            r = span(i, 64)
+            dst[r, :] = dst[r, :] + src[r, :]
+            return 0
+        lax.fori_loop(0, n // 64, body, 0)
+
+    def wait(k, kinds):
+        for kind in kinds:
+            message(k, kind).wait()
+
+    def reduce_stage(k, s):
+        slot = k % RING
+        if s == 0:
+            message(k, 0).start()
+            message(k, 1).start()
+        if s == 1:
+            wait(k, (0, 1))
+            add_into(oth.at[k, c_rows], r1.at[slot, 1], half)
+            message(k, 2).start()
+            add_into(own.at[k, c_rows], r1.at[slot, 0], half)
+        if s == 2:
+            wait(k, (2,))
+            add_into(own.at[k, c_rows], ry.at[slot], half)
+            message(k, 3).start()
+        if s == 3:
+            wait(k, (3,))
+            add_into(own.at[k, x_rows], rx.at[slot], quarter)
+            for kind in (4, 5, 6):
+                message(k, kind).start()
+        if s == 4:
+            wait(k, (4, 5, 6))
+            total = own[k, z_rows(z), :].astype(F32)
+            for d in range(3):
+                total = total + rz[slot, d].astype(F32)
+            oth[k, z_rows(z), :] = total.astype(BF)
+            for kind in (7, 8, 9):
+                message(k, kind).start()
+        if s == 5:
+            wait(k, (7, 8, 9))
+            message(k, 10).start()
+        if s == 6:
+            wait(k, (10,))
+            message(k, 11).start()
+            tile_copy(k).start()
+        if s == 7:
+            wait(k, (11,))
+            tile_copy(k).wait()
+
+    def reduce_step(t):
+        for s in range(8):
+            @pl.when((t >= s) & (t - s < CHUNKS))
+            def _():
+                reduce_stage(t - s, s)
+
+    def small_messages(i):
+        if i == 0:
+            return [copy_to(small, s0, small_send.at[0], small_recv.at[0], to_c)]
+        if i == 1:
+            return [
+                copy_to(small.at[pl.ds(0, 8)], s1.at[pl.ds(0, 8)], small_send.at[1], small_recv.at[1], to_y),
+                copy_to(small.at[pl.ds(16, 8)], s1.at[pl.ds(8, 8)], small_send.at[2], small_recv.at[2], to_y),
+            ]
+        got, peer = ((s2, to_x), (s3, to_zp), (s4, to_zq))[i - 2]
+        return [copy_to(small.at[pl.ds(0, 16)], got, small_send.at[i + 1], small_recv.at[i + 1], peer)]
+
+    def small_step(i):
+        if i > 0:
+            for m in small_messages(i - 1):
+                m.wait()
+            if i == 1:
+                small[...] = small[...] + s0[...]
+            else:
+                small[0:16, :] = small[0:16, :] + (s1, s2, s3, s4)[i - 2][...]
+        if i < 5:
+            for m in small_messages(i):
+                m.start()
+
+    def fetch_ffn(t, start):
+        for h in range(2):
+            @pl.when((t >= 4 * h) & (t < 4 * h + 4))
+            def _():
+                b, a = fetch_in(h, t - 4 * h, t % 3), fetch_down(h, t - 4 * h, t % 2)
+                if start:
+                    b.start()
+                    a.start()
+                else:
+                    b.wait()
+                    a.wait()
+
+    def down_tiles(k):
+        g = gsec[:, span(k % 2, TILE)]
+        own[k] = dot(u1[k // 2], g, 0, 0).astype(BF)
+        oth[k] = dot(u1[4 + k // 2], g, 0, 0).astype(BF)
+
+    def hidden_back(t):
+        fetch_ffn(t, False)
+        g_active = dot(gsec[...], ring_a[t % 2], 1, 1)
+        g_hidden = (g_active * u2[t].astype(F32)).astype(BF)
+        u2[t] = g_hidden
+        total = jnp.sum(g_hidden.astype(F32), axis=0, keepdims=True)
+        small[pl.ds(9 + 8 * (t // 4) + (t % 4) // 2, 1), span(t % 2, TILE)] = total
+        acc[...] += dot(g_hidden, ring_b[t % 3], 1, 1)
+
+    def in_tiles(k):
+        j = k - 8
+        a = nlow[:, span(j % 2, TILE)]
+        own[k] = dot(a, u2[j // 2], 0, 0).astype(BF)
+        oth[k] = dot(a, u2[4 + j // 2], 0, 0).astype(BF)
+
+    def norm_one_back(r, b):
+        g_normed, hat = acc[r, :], xhat[r, :]
+        scaled = g_normed * gain1
+        g_first = rs1[r, 0:1] * (scaled - mean(scaled) - hat * mean(scaled * hat))
+        low = g_first.astype(BF)
+        acc[r, :] = g_first
+        gsec[r, :] = low
+        small[0:1, :] += jnp.sum(g_normed * hat, axis=0, keepdims=True)
+        small[1:2, :] += jnp.sum(g_normed, axis=0, keepdims=True)
+        small[2:3, :] += jnp.sum(low.astype(F32), axis=0, keepdims=True)
+
+    def attend_back(h, p):
+        lanes = span(p, 128)
+        wide = span(h * pairs + p, 128)
+        q2, k2, v2 = qkv[h, 0, :, lanes], qkv[h, 1, :, lanes], qkv[h, 2, :, lanes]
+        g = gctx[:, wide].astype(F32) * inv[h, :, lanes]
+        low = g.astype(BF)
+        less = pltpu.roll(-(g * ctx[:, wide].astype(F32)), HEAD, 1).astype(BF)
+        g_q, g_k, g_v = [], [], []
+        for head in range(2):
+            mine = low_lanes if head == 0 else jnp.logical_not(low_lanes)
+            e = u1[2 * p + head]
+            g_scores = (dot(jnp.where(mine, low, less), jnp.where(mine, v2, one), 1, 1) * e.astype(F32)).astype(BF)
+            g_q.append(dot(g_scores, k2, 1, 0))
+            rows = slice(head * HEAD, head * HEAD + HEAD)
+            g_k.append(dot(q2, g_scores, 0, 0)[rows])
+            g_v.append(dot(low, e, 0, 0)[rows])
+        qkv[h, 0, :, lanes] = (jnp.where(low_lanes, g_q[0], g_q[1]) * scale).astype(BF)
+        qkv[h, 1, :, lanes] = jnp.concatenate(g_k, axis=0).T.astype(BF)
+        qkv[h, 2, :, lanes] = jnp.concatenate(g_v, axis=0).T.astype(BF)
+
+    fetch_ffn(0, True)
+
+    def iteration(t, _):
+        @pl.when(t < 8)
+        def _():
+            down_tiles(t)
+        @pl.when((t >= 8) & (t < 16))
+        def _():
+            in_tiles(t)
+        @pl.when((t >= 16) & (t < 18))
+        def _():
+            g = gsec[:, span(t - 16, TILE)]
+            own[t] = dot(ctx[:, :half_w], g, 0, 0).astype(BF)
+            oth[t] = dot(ctx[:, half_w:], g, 0, 0).astype(BF)
+        @pl.when((t >= 18) & (t < 24))
+        def _():
+            j = t - 18
+            a = xv[:, span(j % 2, TILE)]
+            own[t] = dot(a, qkv[0, j // 2], 0, 0).astype(BF)
+            oth[t] = dot(a, qkv[1, j // 2], 0, 0).astype(BF)
+        reduce_step(t)
+        @pl.when(t < 8)
+        def _():
+            @pl.when(t < 7)
+            def _():
+                fetch_ffn(t + 1, True)
+            hidden_back(t)
+        @pl.when(t == 8)
+        def _():
+            e_copy(0, True).start()
+            fetch_out(0).start()
+            fetch_out(1).start()
+            blocks(norm_one_back)
+        @pl.when(t == 9)
+        def _():
+            out_copy.wait()
+            for h in range(2):
+                fetch_out(h).wait()
+                gctx[:, h * half_w : (h + 1) * half_w] = dot(gsec[...], ring_a[h], 1, 1).astype(BF)
+            e_copy(0, True).wait()
+        for first, h in ((10, 0), (13, 1)):
+            @pl.when((t >= first) & (t < first + 2))
+            def _():
+                def body(p, _):
+                    attend_back(h, 2 * (t - first) + p)
+                    return 0
+                lax.fori_loop(0, 2, body, 0)
+            @pl.when(t == first + 1)
+            def _():
+                if h == 0:
+                    e_copy(1, True).start()
+                for i in (0, 2):
+                    total = jnp.sum(qkv[h, i].astype(F32), axis=0, keepdims=True)
+                    small[8 + 8 * h : 9 + 8 * h, (i // 2) * TILE : (i // 2 + 1) * TILE] = total
+        @pl.when(t == 12)
+        def _():
+            e_copy(1, True).wait()
+        for h in range(2):
+            first = 15 + 2 * h
+            @pl.when(t == first)
+            def _():
+                for i in range(3):
+                    fetch_qkv(h, i).start()
+            @pl.when(t == first + 1)
+            def _():
+                for i in range(3):
+                    fetch_qkv(h, i).wait()
+                    acc[...] += dot(qkv[h, i], ring_b[i], 1, 1)
+        @pl.when(t == 19)
+        def _():
+            def last(r, b):
+                nlow[r, :] = acc[r, :].astype(BF)
+            blocks(last)
+            gin_copy.start()
+        for i in range(6):
+            @pl.when(t == 16 + i)
+            def _():
+                small_step(i)
+        return 0
+
+    lax.fori_loop(0, CHUNKS + 7, iteration, 0)
+    small_out[...] = small[0:16, :]
+    gin_copy.wait()
+
+
+def layer(lengths, inputs, cotangent, wq, w_out, w_in, w_down, vec, bias):
+    seq, width = inputs.shape
+    half = TILE // 2
+    vm, dma = pltpu.VMEM, pltpu.SemaphoreType.DMA
+    anywhere, inside = pl.BlockSpec(memory_space=pl.ANY), pl.BlockSpec(memory_space=pltpu.VMEM)
+    like = lambda a: jax.ShapeDtypeStruct(a.shape, a.dtype)
+    tile_shape = (TILE, TILE)
+    return pl.pallas_call(
+        layer_kernel,
+        out_shape=[
+            like(inputs), like(inputs), jax.ShapeDtypeStruct((CHUNKS,) + tile_shape, BF),
+            jax.ShapeDtypeStruct((16, width), F32),
+            like(wq), like(w_out), like(w_in), like(w_down),
+            jax.ShapeDtypeStruct((16,) + tile_shape, BF),
+        ],
+        in_specs=[pl.BlockSpec(memory_space=pltpu.SMEM)] + [anywhere] * 6 + [inside] * 2,
+        out_specs=[anywhere] * 3 + [inside] + [anywhere] * 5,
+        scratch_shapes=[
+            vm((seq, width), BF), vm((seq, width), BF), vm((seq, width), BF), vm((seq, width), BF), vm((seq, width), BF),
+            vm((2, 3) + tile_shape, BF), vm((2,) + tile_shape, F32),
+            vm((seq, width), F32), vm((seq, 128), F32), vm((seq, width), F32),
+            vm((8,) + tile_shape, BF), vm((8,) + tile_shape, BF),
+            vm((CHUNKS,) + tile_shape, BF), vm((CHUNKS,) + tile_shape, BF),
+            vm((RING, 2, half, TILE), BF), vm((RING, half, TILE), BF),
+            vm((RING, half // 2, TILE), BF), vm((RING, 3, half // 8, TILE), BF),
+            vm((2, TILE, width), BF), vm((3, width, TILE), BF),
+            vm(bias.shape, F32), vm((24, width), F32), vm((24, width), F32),
+            vm((16, width), F32), vm((16, width), F32), vm((16, width), F32), vm((16, width), F32),
+            dma((2,)), dma((2,)), dma((3,)), dma((2,)), dma((2,)), dma((RING,)),
+            dma((9, 10)), dma((9, 10)), dma((RING, MESSAGES)), dma((RING, MESSAGES)), dma((6,)), dma((6,)),
+        ],
+        compiler_params=pltpu.CompilerParams(
+            collective_id=1, has_side_effects=True, vmem_limit_bytes=VMEM_BYTES
+        ),
+    )(lengths, inputs, cotangent, wq, w_out, w_in, w_down, vec, bias)
+
+
+def widen_kernel(tile, down, within, out, three):
+    k = pl.program_id(0)
+    value = tile[...].astype(F32)
+    for ref, first, last in ((down, 0, 8), (within, 8, 16), (out, 16, 18), (three, 18, 24)):
+        @pl.when((k >= first) & (k < last))
+        def _():
+            ref[...] = value
+
+
+def widen(tiles, half_hidden, width, half_width):
+    def within(first, last, place_of):
+        def index(k):
+            return place_of(jnp.clip(k, first, last - 1) - first)
+        return index
+    tile = (TILE, TILE)
+    return pl.pallas_call(
+        widen_kernel,
+        grid=(CHUNKS,),
+        out_shape=[
+            jax.ShapeDtypeStruct((half_hidden, width), F32), jax.ShapeDtypeStruct((width, half_hidden), F32),
+            jax.ShapeDtypeStruct((half_width, width), F32), jax.ShapeDtypeStruct((3, width, half_width), F32),
+        ],
+        in_specs=[pl.BlockSpec((None,) + tile, lambda k: (k, 0, 0))],
+        out_specs=[
+            pl.BlockSpec(tile, within(0, 8, lambda j: (j // 2, j % 2))),
+            pl.BlockSpec(tile, within(8, 16, lambda j: (j % 2, j // 2))),
+            pl.BlockSpec(tile, within(16, 18, lambda j: (0, j))),
+            pl.BlockSpec((None,) + tile, within(18, 24, lambda j: (j // 2, j % 2, 0))),
+        ],
+    )(tiles)
+
+
+def split_by_sequence(
+    inputs, lengths, w_qkv, b_qv, w_out, b_out, gain_one, shift_one, w_in, b_in, w_down, b_down, gain_two, shift_two,
+    cotangent,
+):
+    rows, width = inputs.shape
+    half_width, half_hidden = w_qkv.shape[2], w_in.shape[1]
+    wq = w_qkv.transpose(1, 0, 2)
+    vec = jnp.stack([b_out, gain_one, shift_one, b_down, gain_two, shift_two]).astype(F32)
+    bias = jnp.concatenate([b_qv, b_in.reshape(-1, half_width)], axis=0).astype(F32)
+    output, grad_inputs, tiles, small = layer(lengths, inputs, cotangent, wq, w_out, w_in, w_down, vec, bias)[:4]
+    g_w_down, g_w_in, g_w_out, g_w_qkv = widen(tiles, half_hidden, width, half_width)
+    owned = small[8:].reshape(-1)
+    return (
+        output,
+        grad_inputs,
+        g_w_qkv.transpose(1, 0, 2),
+        owned[: 2 * half_width].reshape(2, half_width),
+        g_w_out,
+        small[2],
+        small[0],
+        small[1],
+        g_w_in,
+        owned[2 * half_width : 2 * half_width + half_hidden],
+        g_w_down,
+        small[5],
+        small[3],
+        small[4],
+    )
+
+
 def solution(mesh):
+    small_mesh = mesh.shape["tensor"] == 2 and mesh.shape["dp"] == 2 * N_X * N_Z
+    step = split_by_sequence if small_mesh else general
     in_specs = (
         P(("dp", "tensor"), None),
         P("dp"),
@@ -331,4 +979,4 @@
         P(),
         P(),
     )
-    return jax.shard_map(local, mesh=mesh, in_specs=in_specs, out_specs=out_specs, check_vma=False)
+    return jax.shard_map(step, mesh=mesh, in_specs=in_specs, out_specs=out_specs, check_vma=False)

time: 831 us -> 291 us (0.35); the launches traced: 822 us -> 290 us
  waiting for transfers between devices: 416 us -> 0 us
  Pallas kernels: 0 us -> 277 us
  matrix products: 185 us -> 0 us
  blocking collectives: 71.2 us -> 0 us
  other arithmetic: 68.3 us -> 1.91 us
  local copies, waits for them, and re-layouts: 63.9 us -> 10.5 us
  between operations: 15.3 us -> 0.67 us
    pallas_call x0 -> x2, Pallas kernels: none -> 277 us  [the longest x1 255 us: layer(): pl.pallas_call(layer_kernel, out_shape=[like(inputs), like(inputs), jax.S...]
    dot_general x30 -> x0, matrix products: 169 us -> none  [the longest x2 35.3 us: forward_pass(): jnp.dot(segment, w_down, preferred_element_type=jnp.float32)]
    psum x1 -> x0, waiting for transfers between devices: 165 us -> none  [local(): lax.psum(grad_w_qkv.astype(jnp.bfloat16), 'dp').astype(jnp.float32)]
    all_gather x5 -> x0, waiting for transfers between devices: 156 us -> none  [the longest x2 56.5 us: forward_pass(): lax.all_gather(normed.astype(jnp.bfloat16), 'tensor', axis=0, tiled=True)]
    reduce_scatter x6 -> x0, waiting for transfers between devices: 93.6 us -> none  [the longest x1 31.9 us: local(): lax.psum_scatter(jnp.einsum('tf,df->td', segment, w_in, preferred_element...]
    psum x2 -> x0, blocking collectives: 71.2 us -> none  [the longest x1 63.7 us: local(): lax.psum(small_terms.astype(jnp.bfloat16), 'dp').astype(jnp.float32)]
    reduce_sum x14 -> x0, other arithmetic: 30 us -> none  [the longest x3 7.81 us: norm_forward(): center = values - jnp.mean(values, axis=-1, keepdims=True)]
    convert_element_type x20 -> x2, other arithmetic: 31.8 us -> 1.91 us  [the longest x1 1.3 us: split_by_sequence(): jnp.concatenate([b_qv, b_in.reshape(-1, half_width)], axis=0).astype(F32)]
  transfers between devices with their start and end apart: 12 -> 0, of which waited for: 9 -> 0; matrix products, arithmetic and copies ran while one was open for 17% -> 0% of each run, Pallas kernels for 0% -> 0%
where the time goes in v2:
time: 291 us; the launch traced here: 290 us
  Pallas kernels  277 us (95%)
  local copies, waits for them, and re-layouts  10.5 us (4%)
    pallas_call x1, Pallas kernels, layer(): pl.pallas_call(layer_kernel, out_shape=[like(inputs), like(inputs), jax.S...  255 us
    pallas_call x1, Pallas kernels, widen(): pl.pallas_call(widen_kernel, grid=(CHUNKS,), out_shape=[jax.ShapeDtypeStr...  21.9 us

profile of v2, /device:TPU:0, one launch (start us, length us, event | category | flops | bytes accessed | tf_op | source)
XLA Modules:
  0.0 290.1 jit_solution(13409543395807015983)
XLA Ops:
  0.6 0.7 stack.21
  1.3 0.7 stack.22
  2.0 0.7 stack.23
  2.7 0.7 reshape.38
  3.4 0.7 stack.24
  4.1 0.7 stack.25
  4.8 0.7 stack.26
  5.5 1.3 maximum_convert_fusion.bias_own
  6.8 0.6 convert_element_type.6.vec
  7.4 255.2 %shard_map.254 = (bf16[512,1024]{1,0:T(8,128)(2,1)}, bf16[512,1024]{1,0:T(8,128)(2,1)}, bf16[24,512,512]{2,1,0:T(8,128)(2,1)}, f32[16,1024]{1,0:T(8,128)}, bf16[...) custom-call(s32[2]{0:T(128)} %lengths.1, ...), custom_call_target="tpu_custom_call" | custom-call | tf_op jit(solution)/shard_map/pallas_call | solution.py:854
  262.6 0.8 slice_bitcast_fusion
  263.4 1.7 fusion
  265.1 0.6 copy.31
  265.7 0.6 reshape.39
  266.3 0.0 copy-start.1
  266.3 0.0 copy-start
  266.3 21.9 %shard_map.255 = (f32[2048,1024]{1,0:T(8,128)}, f32[1024,2048]{1,0:T(8,128)}, f32[512,1024]{1,0:T(8,128)}, f32[3,1024,512]{2,1,0:T(8,128)}) custom-call(bf16[24,512,512]{2,1,0:T(8,128)(2,1)} %get-tuple-element.24.tile), custom_call_target="tpu_custom_call" | custom-call | tf_op jit(solution)/shard_map/pallas_call | solution.py:899
  288.2 0.0 copy-done.1
  288.2 1.0 copy.34
  289.1 0.0 copy-done
  289.2 1.0 copy.35
  (1 shorter events, 0.0 us)
Async XLA Ops:
  266.3 21.9 %copy-start.1 = (bf16[512,1024]{1,0:T(8,128)(2,1)S(1)}, bf16[512,1024]{1,0:T(8,128)(2,1)}, u32[]{:S(2)}) copy-start(bf16[512,1024]{1,0:T(8,128)(2,1)} %get-tuple-element.51) | copy-start | bytes 3145732
  266.3 22.9 %copy-start = (bf16[512,1024]{1,0:T(8,128)(2,1)S(1)}, bf16[512,1024]{1,0:T(8,128)(2,1)}, u32[]{:S(2)}) copy-start(bf16[512,1024]{1,0:T(8,128)(2,1)} %get-tuple-element.52) | copy-start | bytes 3145732

commit v3 on v2

--- a/solution.py
+++ b/solution.py
@@ -331,7 +331,7 @@
 CHUNKS = 24
 RING = 4
 BF, F32 = jnp.bfloat16, jnp.float32
-ROWS_AT_ONCE = 32
+ROWS_AT_ONCE = 64
 
 
 def dot(a, b, ca, cb):
@@ -342,12 +342,25 @@
     return pl.ds(pl.multiple_of(index * size, size), size)
 
 
+def tile_place(k):
+    if k < 8:
+        return 0, (slice(k // 2 * TILE, (k // 2 + 1) * TILE), slice(k % 2 * TILE, (k % 2 + 1) * TILE))
+    if k < 16:
+        k -= 8
+        return 1, (slice(k % 2 * TILE, (k % 2 + 1) * TILE), slice(k // 2 * TILE, (k // 2 + 1) * TILE))
+    if k < 18:
+        k -= 16
+        return 2, (slice(0, TILE), slice(k * TILE, (k + 1) * TILE))
+    k -= 18
+    return 3, (k // 2, slice(k % 2 * TILE, (k % 2 + 1) * TILE), slice(0, TILE))
+
+
 def layer_kernel(
-    lengths, x_hbm, cot_hbm, wq_own, wo_own, wi_own, wd_own, vec, bias_own,
+    lengths, x_hbm, cot_hbm, wq_own, wo_own, wi_own, wd_own, in1, in2, in3, in4, in5, in6, in_qv, in_hidden,
     out_hbm, gin_hbm, tiles_hbm, small_out, wq_oth, wo_oth, wi_oth, wd_oth, e_hbm,
     xv, nlow, gsec, gctx, ctx, qkv, inv, xhat, rs1, acc, u1, u2, own, oth, r1, ry, rx, rz,
-    ring_a, ring_b, bias_oth, small, s0, s1, s2, s3, s4,
-    load_sem, a_sem, b_sem, e_sem, o_sem, t_sem, g_send, g_recv, send, recv, small_send, small_recv,
+    ring_a, ring_b, vec, bias_own, bias_oth, small, s0, s1, s2, s3, s4,
+    load_sem, w_sem, a_sem, b_sem, e_sem, o_sem, t_sem, g_send, g_recv, send, recv, small_send, small_recv,
 ):
     z, x, c, y = place()
     zb = z % 2
@@ -362,6 +375,10 @@
     load_cot = pltpu.make_async_copy(cot_hbm, gsec, load_sem.at[1])
     load_x.start()
     load_cot.start()
+    for row, ref in enumerate((in1, in2, in3, in4, in5, in6)):
+        vec[row : row + 1, :] = ref[...].astype(F32).reshape(1, width)
+    bias_own[0:2, :] = in_qv[...].astype(F32)
+    bias_own[2:6, :] = in_hidden[...].astype(F32).reshape(4, TILE)
 
     def fetch_qkv(h, i):
         source = (wq_own, wq_oth)[h]
@@ -376,31 +393,38 @@
     def fetch_down(h, f, slot):
         return pltpu.make_async_copy((wd_own, wd_oth)[h].at[span(f, TILE)], ring_a.at[slot], a_sem.at[slot])
 
-    for i in range(3):
-        fetch_qkv(0, i).start()
-    fetch_out(0).start()
+    def weight_load(h, k):
+        which, where = tile_place(k)
+        source = ((wd_own, wi_own, wo_own, wq_own), (wd_oth, wi_oth, wo_oth, wq_oth))[h][which]
+        return pltpu.make_async_copy(source.at[where], (own, oth)[h].at[k], w_sem.at[h, k])
+
+    for k in (*range(18, 24), *range(8, 16), *range(0, 8), 16, 17):
+        weight_load(0, k).start()
 
     greet([to_c, to_y, to_x] + to_z)
 
     cut = wi_own.shape[1] // 2
     deep = wd_own.shape[0] // 2
     arrays = [(wq_own.at[i], wq_oth.at[i]) for i in range(3)] + [(wo_own, wo_oth)]
-    for j in range(2):
-        arrays.append((wi_own.at[:, j * cut : (j + 1) * cut], wi_oth.at[:, j * cut : (j + 1) * cut]))
-        arrays.append((wd_own.at[j * deep : (j + 1) * deep], wd_oth.at[j * deep : (j + 1) * deep]))
+    arrays += [(wi_own.at[:, j * cut : (j + 1) * cut], wi_oth.at[:, j * cut : (j + 1) * cut]) for j in range(2)]
+    arrays += [(wd_own.at[j * deep : (j + 1) * deep], wd_oth.at[j * deep : (j + 1) * deep]) for j in range(2)]
+    loads_of = [(18, 19), (20, 21), (22, 23), (16, 17), (8, 9, 10, 11), (12, 13, 14, 15), (0, 1, 2, 3), (4, 5, 6, 7)]
     count = len(arrays)
 
     def gather_message(n, kind):
-        size = arrays[n][0].shape[0] // 16
-        pair_a, pair_b = (0, 2 * zb, 2), (1, 2 * x, 2)
-        one_a, one_b = (0, 2 * zb + x, 1), (1, 2 * x + zb, 1)
-        far_a, far_b = (0, 2 * (1 - zb), 2), (1, 2 * (1 - x), 2)
-        (group, first, parts), peer = [
-            (one_a, to_y), (one_b, to_y), (one_a, to_x), (one_b, to_zp),
-            (pair_a, to_zp), (pair_b, to_x), (pair_a, to_c), (pair_b, to_c), (far_a, to_c), (far_b, to_c),
+        size = arrays[n][0].shape[0] // 2
+        size_part = size // 8 - (8 if n >= 4 else 0)
+        near_a, near_b = 2 * zb, 4 + 2 * x
+        far_a, far_b = 2 * (1 - zb), 4 + 2 * (1 - x)
+        one_a, one_b = 2 * zb + x, 4 + 2 * x + zb
+        first, parts, peer = [
+            (one_a, 1, to_y), (one_b, 1, to_y), (one_a, 1, to_x), (one_b, 1, to_zp),
+            (near_a, 2, to_zp), (near_b, 2, to_x), (near_a, 2, to_c), (near_b, 2, to_c), (far_a, 2, to_c), (far_b, 2, to_c),
+            (8, 0, to_y), (8, 0, to_c),
         ][kind]
-        rows = pl.ds(pl.multiple_of(c * 8 * size + group * 4 * size + first * size, 16), parts * size)
-        source = arrays[n][0 if kind < 2 else 1]
+        length_rows = parts * size_part if parts else size - 8 * size_part
+        rows = pl.ds(pl.multiple_of(c * size + first * size_part, 8), length_rows)
+        source = arrays[n][0 if kind in (0, 1, 10) else 1]
         return copy_to(source.at[rows], arrays[n][1].at[rows], g_send.at[n, kind], g_recv.at[n, kind], peer)
 
     def gather_stage(n, step):
@@ -421,10 +445,17 @@
             gather_message(n, 8).start()
             gather_message(n, 5).wait_recv()
             gather_message(n, 9).start()
+            if n >= 4:
+                gather_message(n, 10).wait_recv()
+                gather_message(n, 11).start()
         if step == 3:
-            for kind in (6, 7, 8, 9):
-                gather_message(n, kind).wait_recv()
-            for kind in range(10):
+            kinds = range(12 if n >= 4 else 10)
+            for kind in kinds:
+                if kind >= 6 and kind != 10:
+                    gather_message(n, kind).wait_recv()
+            for k in loads_of[n]:
+                weight_load(1, k).start()
+            for kind in kinds:
                 gather_message(n, kind).wait_send()
 
     def progress(slot):
@@ -434,9 +465,9 @@
 
     send_bias = copy_to(bias_own, bias_oth, g_send.at[count, 0], g_recv.at[count, 0], to_y)
     send_bias.start()
-    for n in range(count):
-        gather_message(n, 0).start()
-        gather_message(n, 1).start()
+    for n in (0, 1, 2, 3, 4, 5, -4, 6, -5, 7, -6, -7):
+        for kind in (0, 1) if n >= 0 else (10,):
+            gather_message(abs(n), kind).start()
 
     length = lengths[y]
     key_fill = jnp.where(lax.broadcasted_iota(jnp.int32, (1, seq), 1) < length, 0.0, NEG_FILL)
@@ -448,8 +479,9 @@
     def project(h):
         bias = (bias_own, bias_oth)[h]
         for i in range(3):
-            fetch_qkv(h, i).wait()
-            value = dot(xv[...], ring_b[i], 1, 0)
+            for k in (18 + 2 * i, 19 + 2 * i):
+                weight_load(h, k).wait()
+            value = dot(xv[...], (own, oth)[h][18 + 2 * i : 20 + 2 * i].reshape(width, TILE), 1, 0)
             if i == 0:
                 qkv[h, 0] = (value + bias[0:1, :]).astype(BF) * jnp.asarray(scale, BF)
             if i == 1:
@@ -487,29 +519,25 @@
         ref, buf = e_hbm.at[pl.ds(h * 8, 8)], (u1 if back else (u1, u2)[h])
         return pltpu.make_async_copy(ref, buf, e_sem.at[h]) if back else pltpu.make_async_copy(buf, ref, e_sem.at[h])
 
+    def out_project(h):
+        for d in range(2):
+            weight_load(h, 16 + d).wait()
+            term = dot(ctx[:, h * half_w : (h + 1) * half_w], (own, oth)[h][16 + d], 1, 0)
+            lanes = slice(d * TILE, (d + 1) * TILE)
+            acc[:, lanes] = term if h == 0 else acc[:, lanes] + term
+
     load_x.wait()
     project(0)
     attend_half(0, ((1, 0), (3, 1)))
     e_copy(0, False).start()
-    fetch_out(0).wait()
-    acc[...] = dot(ctx[:, :half_w], ring_a[0], 1, 0)
-    for slot in (2, 3):
+    out_project(0)
+    for slot in (2, 3, 4, 5):
         progress(slot)
     send_bias.wait()
-    fetch_qkv(1, 0).start()
-    progress(4)
-    fetch_qkv(1, 1).start()
-    progress(5)
-    fetch_qkv(1, 2).start()
     project(1)
-    attend_half(1, ((2, 6),))
+    attend_half(1, ((1, 6),))
     e_copy(1, False).start()
-    fetch_out(1).start()
-    for f in range(2):
-        fetch_in(0, f, f).start()
-    fetch_down(0, 0, 0).start()
-    fetch_out(1).wait()
-    acc[...] += dot(ctx[:, half_w:], ring_a[1], 1, 0)
+    out_project(1)
     progress(7)
 
     def blocks(body):
@@ -534,40 +562,35 @@
         rs1[r, :] = jnp.broadcast_to(inverse, (ROWS_AT_ONCE, 128))
         nlow[r, :] = (hat * gain1 + shift1).astype(BF)
     blocks(norm_one)
-    acc[...] = jnp.zeros_like(acc)
     e_copy(0, False).wait()
     e_copy(1, False).wait()
 
     def hidden_half(h, slots):
-        bias = (bias_own, bias_oth)[h]
-        def body(f, _):
-            t = h * 4 + f
-            b_slot, a_slot = t % 3, t % 2
-            @pl.when(f + 2 < 4)
-            def _():
-                fetch_in(h, f + 2, (t + 2) % 3).start()
-            @pl.when(f + 1 < 4)
-            def _():
-                fetch_down(h, f + 1, (t + 1) % 2).start()
-            fetch_in(h, f, b_slot).wait()
-            hidden = dot(nlow[...], ring_b[b_slot], 1, 0) + bias[pl.ds(2 + f, 1), :]
+        bias, weights = (bias_own, bias_oth)[h], (own, oth)[h]
+        for f in range(4):
+            for k in (8 + 2 * f, 9 + 2 * f):
+                weight_load(h, k).wait()
+            hidden = dot(nlow[...], weights[8 + 2 * f : 10 + 2 * f].reshape(width, TILE), 1, 0) + bias[2 + f : 3 + f, :]
             cdf = 0.5 + 0.5 * lax.erf(hidden * 0.7071067811865476)
-            u1[t] = (hidden * cdf).astype(BF)
-            u2[t] = (cdf + hidden * (jnp.exp(hidden * hidden * -0.5) * 0.3989422804014327)).astype(BF)
-            fetch_down(h, f, a_slot).wait()
-            acc[...] += dot(u1[t], ring_a[a_slot], 1, 0)
-            for at_tile, slot in slots:
-                @pl.when(f == at_tile)
-                def _():
-                    progress(slot)
-            return 0
-        lax.fori_loop(0, 4, body, 0)
-
-    hidden_half(0, ((0, 8), (2, 9)))
-    for g in range(2):
-        fetch_in(1, g, (4 + g) % 3).start()
-    fetch_down(1, 0, 0).start()
-    hidden_half(1, ((0, 10),))
+            u1[4 * h + f] = (hidden * cdf).astype(BF)
+            u2[4 * h + f] = (cdf + hidden * (jnp.exp(hidden * hidden * -0.5) * 0.3989422804014327)).astype(BF)
+            if f in slots:
+                progress(slots[f])
+
+    def down_half(h, tiles, clear=False):
+        for f in tiles:
+            for d in range(2):
+                weight_load(h, 2 * f + d).wait()
+                term = dot(u1[4 * h + f], (own, oth)[h][2 * f + d], 1, 0)
+                lanes = slice(d * TILE, (d + 1) * TILE)
+                acc[:, lanes] = term if clear and f == tiles[0] else acc[:, lanes] + term
+
+    hidden_half(0, {2: 8})
+    down_half(0, (0, 1, 2, 3), True)
+    hidden_half(1, {1: 9})
+    down_half(1, (0, 1))
+    progress(10)
+    down_half(1, (2, 3))
 
     load_cot.wait()
     valid_limit = lengths[y]
@@ -844,7 +867,7 @@
     gin_copy.wait()
 
 
-def layer(lengths, inputs, cotangent, wq, w_out, w_in, w_down, vec, bias):
+def layer(lengths, inputs, cotangent, wq, w_out, w_in, w_down, vectors):
     seq, width = inputs.shape
     half = TILE // 2
     vm, dma = pltpu.VMEM, pltpu.SemaphoreType.DMA
@@ -859,7 +882,7 @@
             like(wq), like(w_out), like(w_in), like(w_down),
             jax.ShapeDtypeStruct((16,) + tile_shape, BF),
         ],
-        in_specs=[pl.BlockSpec(memory_space=pltpu.SMEM)] + [anywhere] * 6 + [inside] * 2,
+        in_specs=[pl.BlockSpec(memory_space=pltpu.SMEM)] + [anywhere] * 6 + [inside] * 8,
         out_specs=[anywhere] * 3 + [inside] + [anywhere] * 5,
         scratch_shapes=[
             vm((seq, width), BF), vm((seq, width), BF), vm((seq, width), BF), vm((seq, width), BF), vm((seq, width), BF),
@@ -870,47 +893,74 @@
             vm((RING, 2, half, TILE), BF), vm((RING, half, TILE), BF),
             vm((RING, half // 2, TILE), BF), vm((RING, 3, half // 8, TILE), BF),
             vm((2, TILE, width), BF), vm((3, width, TILE), BF),
-            vm(bias.shape, F32), vm((24, width), F32), vm((24, width), F32),
+            vm((8, width), F32), vm((8, TILE), F32), vm((8, TILE), F32), vm((24, width), F32), vm((24, width), F32),
             vm((16, width), F32), vm((16, width), F32), vm((16, width), F32), vm((16, width), F32),
-            dma((2,)), dma((2,)), dma((3,)), dma((2,)), dma((2,)), dma((RING,)),
-            dma((9, 10)), dma((9, 10)), dma((RING, MESSAGES)), dma((RING, MESSAGES)), dma((6,)), dma((6,)),
+            dma((2,)), dma((2, CHUNKS)), dma((2,)), dma((3,)), dma((2,)), dma((2,)), dma((RING,)),
+            dma((9, 12)), dma((9, 12)), dma((RING, MESSAGES)), dma((RING, MESSAGES)), dma((6,)), dma((6,)),
         ],
         compiler_params=pltpu.CompilerParams(
             collective_id=1, has_side_effects=True, vmem_limit_bytes=VMEM_BYTES
         ),
-    )(lengths, inputs, cotangent, wq, w_out, w_in, w_down, vec, bias)
-
-
-def widen_kernel(tile, down, within, out, three):
-    k = pl.program_id(0)
-    value = tile[...].astype(F32)
-    for ref, first, last in ((down, 0, 8), (within, 8, 16), (out, 16, 18), (three, 18, 24)):
-        @pl.when((k >= first) & (k < last))
-        def _():
-            ref[...] = value
-
-
-def widen(tiles, half_hidden, width, half_width):
-    def within(first, last, place_of):
-        def index(k):
-            return place_of(jnp.clip(k, first, last - 1) - first)
-        return index
-    tile = (TILE, TILE)
+    )(lengths, inputs, cotangent, wq, w_out, w_in, w_down, *vectors)
+
+
+def widen_kernel(
+    tiles, out_in, gin_in, sums, down, within, out, three, out_out, gin_out,
+    b_qv, b_out, gain1, shift1, b_in, b_down, gain2, shift2, low, wide, held, in_sem, out_sem, pass_sem,
+):
+    enter = [pltpu.make_async_copy(ref, held.at[i], pass_sem.at[i]) for i, ref in enumerate((out_in, gin_in))]
+    leave = [pltpu.make_async_copy(held.at[i], ref, pass_sem.at[i]) for i, ref in enumerate((out_out, gin_out))]
+    loads = [pltpu.make_async_copy(tiles.at[k], low.at[k], in_sem.at[k]) for k in range(CHUNKS)]
+    for copy in loads[:RING] + enter + loads[RING:]:
+        copy.start()
+    width, half = sums.shape[1], b_qv.shape[1]
+    for ref, row in ((gain1, 0), (shift1, 1), (b_out, 2), (gain2, 3), (shift2, 4), (b_down, 5)):
+        ref[...] = sums[row, :]
+    for i in range(2):
+        b_qv[i : i + 1, :] = sums[8:9, i * half : (i + 1) * half]
+        b_in[i * width : (i + 1) * width] = sums[9 + i, :]
+
+    def store(k):
+        which, where = tile_place(k)
+        return pltpu.make_async_copy(wide.at[k % RING], (down, within, out, three)[which].at[where], out_sem.at[k % RING])
+
+    stores = [store(k) for k in range(CHUNKS)]
+    for k in range(CHUNKS):
+        loads[k].wait()
+        if k >= RING:
+            stores[k - RING].wait()
+        def body(i, _):
+            r = span(i, 32)
+            wide[k % RING, r, :] = low[k, r, :].astype(F32)
+            return 0
+        lax.fori_loop(0, TILE // 32, body, 0)
+        stores[k].start()
+        if k == RING:
+            for into, back in zip(enter, leave):
+                into.wait()
+                back.start()
+    for copy in stores[CHUNKS - RING :] + leave:
+        copy.wait()
+
+
+def widen(tiles, output, grad_inputs, sums, half_hidden, width, half_width):
+    tile, vm, dma = (TILE, TILE), pltpu.VMEM, pltpu.SemaphoreType.DMA
+    anywhere, inside = pl.BlockSpec(memory_space=pl.ANY), pl.BlockSpec(memory_space=pltpu.VMEM)
+    wide = lambda *shape: jax.ShapeDtypeStruct(shape, F32)
     return pl.pallas_call(
         widen_kernel,
-        grid=(CHUNKS,),
         out_shape=[
-            jax.ShapeDtypeStruct((half_hidden, width), F32), jax.ShapeDtypeStruct((width, half_hidden), F32),
-            jax.ShapeDtypeStruct((half_width, width), F32), jax.ShapeDtypeStruct((3, width, half_width), F32),
+            wide(half_hidden, width), wide(width, half_hidden), wide(half_width, width), wide(3, width, half_width),
+            jax.ShapeDtypeStruct(output.shape, output.dtype), jax.ShapeDtypeStruct(output.shape, output.dtype),
+            wide(2, half_width), wide(width), wide(width), wide(width), wide(half_hidden), wide(width), wide(width), wide(width),
         ],
-        in_specs=[pl.BlockSpec((None,) + tile, lambda k: (k, 0, 0))],
-        out_specs=[
-            pl.BlockSpec(tile, within(0, 8, lambda j: (j // 2, j % 2))),
-            pl.BlockSpec(tile, within(8, 16, lambda j: (j % 2, j // 2))),
-            pl.BlockSpec(tile, within(16, 18, lambda j: (0, j))),
-            pl.BlockSpec((None,) + tile, within(18, 24, lambda j: (j // 2, j % 2, 0))),
+        in_specs=[anywhere] * 3 + [inside],
+        out_specs=[anywhere] * 6 + [inside] * 8,
+        scratch_shapes=[
+            vm((CHUNKS,) + tile, BF), vm((RING,) + tile, F32), vm((2,) + output.shape, BF), dma((CHUNKS,)), dma((RING,)), dma((2,)),
         ],
-    )(tiles)
+        compiler_params=pltpu.CompilerParams(vmem_limit_bytes=60 << 20),
+    )(tiles, output, grad_inputs, sums)
 
 
 def split_by_sequence(
@@ -920,26 +970,16 @@
     rows, width = inputs.shape
     half_width, half_hidden = w_qkv.shape[2], w_in.shape[1]
     wq = w_qkv.transpose(1, 0, 2)
-    vec = jnp.stack([b_out, gain_one, shift_one, b_down, gain_two, shift_two]).astype(F32)
-    bias = jnp.concatenate([b_qv, b_in.reshape(-1, half_width)], axis=0).astype(F32)
-    output, grad_inputs, tiles, small = layer(lengths, inputs, cotangent, wq, w_out, w_in, w_down, vec, bias)[:4]
-    g_w_down, g_w_in, g_w_out, g_w_qkv = widen(tiles, half_hidden, width, half_width)
-    owned = small[8:].reshape(-1)
+    vectors = (b_out, gain_one, shift_one, b_down, gain_two, shift_two, b_qv, b_in)
+    made = layer(lengths, inputs, cotangent, wq, w_out, w_in, w_down, vectors)
+    output, grad_inputs, tiles, sums = made[:4]
+    (
+        g_w_down, g_w_in, g_w_out, g_w_qkv, output, grad_inputs,
+        g_b_qv, g_b_out, g_gain_one, g_shift_one, g_b_in, g_b_down, g_gain_two, g_shift_two,
+    ) = widen(tiles, output, grad_inputs, sums, half_hidden, width, half_width)
     return (
-        output,
-        grad_inputs,
-        g_w_qkv.transpose(1, 0, 2),
-        owned[: 2 * half_width].reshape(2, half_width),
-        g_w_out,
-        small[2],
-        small[0],
-        small[1],
-        g_w_in,
-        owned[2 * half_width : 2 * half_width + half_hidden],
-        g_w_down,
-        small[5],
-        small[3],
-        small[4],
+        output, grad_inputs, g_w_qkv.transpose(1, 0, 2), g_b_qv, g_w_out, g_b_out, g_gain_one, g_shift_one,
+        g_w_in, g_b_in, g_w_down, g_b_down, g_gain_two, g_shift_two,
     )
 
 

time: 291 us -> 266 us (0.914)
  Pallas kernels: 277 us -> 265 us
  local copies, waits for them, and re-layouts: 10.5 us -> 0 us
    pallas_call x1, Pallas kernels: 21.9 us -> 15.8 us  [widen(): pl.pallas_call(widen_kernel, out_shape=[wide(half_hidden, width), wide(wi...]
    pallas_call x1, Pallas kernels: 255 us -> 250 us  [layer(): pl.pallas_call(layer_kernel, out_shape=[like(inputs), like(inputs), jax.S...]
    another operation x7 -> x0, local copies, waits for them, and re-layouts: 4.16 us -> none  [split_by_sequence(): jnp.stack([b_out, gain_one, shift_one, b_down, gain_two, shift_two])]
    unnamed x8 -> x0, local copies, waits for them, and re-layouts: 3.31 us -> none
where the time goes in v3:
time: 266 us
  Pallas kernels  265 us (100%)
    pallas_call x1, Pallas kernels, layer(): pl.pallas_call(layer_kernel, out_shape=[like(inputs), like(inputs), jax.S...  250 us
    pallas_call x1, Pallas kernels, widen(): pl.pallas_call(widen_kernel, out_shape=[wide(half_hidden, width), wide(wi...  15.8 us

profile of v3, /device:TPU:0, one launch (start us, length us, event | category | flops | bytes accessed | tf_op | source)
XLA Modules:
  0.0 266.1 jit_solution(1683634855315919851)
XLA Ops:
  0.7 249.5 %shard_map.254 = (bf16[512,1024]{1,0:T(8,128)(2,1)}, bf16[512,1024]{1,0:T(8,128)(2,1)}, bf16[24,512,512]{2,1,0:T(8,128)(2,1)}, f32[16,1024]{1,0:T(8,128)}, bf16[...) custom-call(s32[2]{0:T(128)} %lengths.1, ...), custom_call_target="tpu_custom_call" | custom-call | tf_op jit(solution)/shard_map/pallas_call | solution.py:877
  250.2 15.8 %shard_map.255 = (f32[2048,1024]{1,0:T(8,128)}, f32[1024,2048]{1,0:T(8,128)}, f32[512,1024]{1,0:T(8,128)}, f32[3,1024,512]{2,1,0:T(8,128)}, bf16[512,1024]{1,0:T...) custom-call(bf16[24,512,512]{2,1,0:T(8,128)(2,1)} %get-tuple-element, ...), custom_call_target="tpu_custom_call" | custom-call | tf_op jit(solution)/shard_map/pallas_call | solution.py:950

commit v4 on v3

--- a/solution.py
+++ b/solution.py
@@ -357,10 +357,10 @@
 
 def layer_kernel(
     lengths, x_hbm, cot_hbm, wq_own, wo_own, wi_own, wd_own, in1, in2, in3, in4, in5, in6, in_qv, in_hidden,
-    out_hbm, gin_hbm, tiles_hbm, small_out, wq_oth, wo_oth, wi_oth, wd_oth, e_hbm,
-    xv, nlow, gsec, gctx, ctx, qkv, inv, xhat, rs1, acc, u1, u2, own, oth, r1, ry, rx, rz,
+    out_ref, gin_ref, oth, small_out, wq_oth, wo_oth, wi_oth, wd_oth, e_hbm,
+    xv, nlow, gsec, gctx, ctx, qkv, inv, xhat, rs1, acc, u1, u2, own, r1, ry, rx, rz,
     ring_a, ring_b, vec, bias_own, bias_oth, small, s0, s1, s2, s3, s4,
-    load_sem, w_sem, a_sem, b_sem, e_sem, o_sem, t_sem, g_send, g_recv, send, recv, small_send, small_recv,
+    load_sem, w_sem, a_sem, b_sem, e_sem, g_send, g_recv, send, recv, small_send, small_recv,
 ):
     z, x, c, y = place()
     zb = z % 2
@@ -538,7 +538,6 @@
     attend_half(1, ((1, 6),))
     e_copy(1, False).start()
     out_project(1)
-    progress(7)
 
     def blocks(body):
         def run(b, _):
@@ -564,6 +563,7 @@
     blocks(norm_one)
     e_copy(0, False).wait()
     e_copy(1, False).wait()
+    progress(7)
 
     def hidden_half(h, slots):
         bias, weights = (bias_own, bias_oth)[h], (own, oth)[h]
@@ -585,9 +585,11 @@
                 lanes = slice(d * TILE, (d + 1) * TILE)
                 acc[:, lanes] = term if clear and f == tiles[0] else acc[:, lanes] + term
 
-    hidden_half(0, {2: 8})
-    down_half(0, (0, 1, 2, 3), True)
-    hidden_half(1, {1: 9})
+    hidden_half(0, {})
+    down_half(0, (0, 1), True)
+    progress(8)
+    down_half(0, (2, 3))
+    hidden_half(1, {3: 9})
     down_half(1, (0, 1))
     progress(10)
     down_half(1, (2, 3))
@@ -601,7 +603,7 @@
         center = v - mean(v)
         inverse = lax.rsqrt(mean(center * center) + EPSILON)
         hat = center * inverse
-        gctx[r, :] = (hat * gain2 + shift2).astype(BF)
+        out_ref[r, :] = (hat * gain2 + shift2).astype(BF)
         position = b * ROWS_AT_ONCE + lax.broadcasted_iota(jnp.int32, (ROWS_AT_ONCE, 1), 0)
         g_out = jnp.where(position < valid_limit, gsec[r, :].astype(F32), 0.0)
         scaled = g_out * gain2
@@ -613,9 +615,6 @@
         small[4:5, :] += jnp.sum(g_out, axis=0, keepdims=True)
         small[5:6, :] += jnp.sum(low.astype(F32), axis=0, keepdims=True)
     blocks(norm_two)
-    out_copy = pltpu.make_async_copy(gctx, out_hbm, o_sem.at[0])
-    gin_copy = pltpu.make_async_copy(nlow, gin_hbm, o_sem.at[1])
-    out_copy.start()
 
     half, quarter, part = TILE // 2, TILE // 4, TILE // 16
     c_rows = span(c, half)
@@ -635,11 +634,8 @@
         if 4 <= kind < 7: src, dst, peer = own.at[k, z_rows(z_of[kind - 4])], rz.at[slot, kind - 4], to_z[kind - 4]
         if 7 <= kind < 10: src, dst, peer = oth.at[k, z_rows(z)], oth.at[k, z_rows(z)], to_z[kind - 7]
         if kind == 10: src, dst, peer = oth.at[k, x_rows], oth.at[k, x_rows], to_x
-        if kind == 11: src, dst, peer = oth.at[k, c_rows], tiles_hbm.at[k, c_rows], to_c
+        if kind == 11: src, dst, peer = oth.at[k, c_rows], oth.at[k, c_rows], to_c
         return copy_to(src, dst, send.at[slot, kind], recv.at[slot, kind], peer)
-
-    def tile_copy(k):
-        return pltpu.make_async_copy(oth.at[k, c_rows], tiles_hbm.at[k, c_rows], t_sem.at[k % RING])
 
     def add_into(dst, src, n):
         def body(i, _):
@@ -685,10 +681,8 @@
         if s == 6:
             wait(k, (10,))
             message(k, 11).start()
-            tile_copy(k).start()
         if s == 7:
             wait(k, (11,))
-            tile_copy(k).wait()
 
     def reduce_step(t):
         for s in range(8):
@@ -817,7 +811,6 @@
             blocks(norm_one_back)
         @pl.when(t == 9)
         def _():
-            out_copy.wait()
             for h in range(2):
                 fetch_out(h).wait()
                 gctx[:, h * half_w : (h + 1) * half_w] = dot(gsec[...], ring_a[h], 1, 1).astype(BF)
@@ -853,9 +846,8 @@
         @pl.when(t == 19)
         def _():
             def last(r, b):
-                nlow[r, :] = acc[r, :].astype(BF)
+                gin_ref[r, :] = acc[r, :].astype(BF)
             blocks(last)
-            gin_copy.start()
         for i in range(6):
             @pl.when(t == 16 + i)
             def _():
@@ -864,7 +856,6 @@
 
     lax.fori_loop(0, CHUNKS + 7, iteration, 0)
     small_out[...] = small[0:16, :]
-    gin_copy.wait()
 
 
 def layer(lengths, inputs, cotangent, wq, w_out, w_in, w_down, vectors):
@@ -877,41 +868,39 @@
     return pl.pallas_call(
         layer_kernel,
         out_shape=[
-            like(inputs), like(inputs), jax.ShapeDtypeStruct((CHUNKS,) + tile_shape, BF),
-            jax.ShapeDtypeStruct((16, width), F32),
+            pltpu.VMEM(inputs.shape, BF), pltpu.VMEM(inputs.shape, BF), pltpu.VMEM((CHUNKS,) + tile_shape, BF),
+            pltpu.VMEM((16, width), F32),
             like(wq), like(w_out), like(w_in), like(w_down),
             jax.ShapeDtypeStruct((16,) + tile_shape, BF),
         ],
         in_specs=[pl.BlockSpec(memory_space=pltpu.SMEM)] + [anywhere] * 6 + [inside] * 8,
-        out_specs=[anywhere] * 3 + [inside] + [anywhere] * 5,
+        out_specs=[inside] * 4 + [anywhere] * 5,
         scratch_shapes=[
             vm((seq, width), BF), vm((seq, width), BF), vm((seq, width), BF), vm((seq, width), BF), vm((seq, width), BF),
             vm((2, 3) + tile_shape, BF), vm((2,) + tile_shape, F32),
             vm((seq, width), F32), vm((seq, 128), F32), vm((seq, width), F32),
             vm((8,) + tile_shape, BF), vm((8,) + tile_shape, BF),
-            vm((CHUNKS,) + tile_shape, BF), vm((CHUNKS,) + tile_shape, BF),
+            vm((CHUNKS,) + tile_shape, BF),
             vm((RING, 2, half, TILE), BF), vm((RING, half, TILE), BF),
             vm((RING, half // 2, TILE), BF), vm((RING, 3, half // 8, TILE), BF),
             vm((2, TILE, width), BF), vm((3, width, TILE), BF),
             vm((8, width), F32), vm((8, TILE), F32), vm((8, TILE), F32), vm((24, width), F32), vm((24, width), F32),
             vm((16, width), F32), vm((16, width), F32), vm((16, width), F32), vm((16, width), F32),
-            dma((2,)), dma((2, CHUNKS)), dma((2,)), dma((3,)), dma((2,)), dma((2,)), dma((RING,)),
+            dma((2,)), dma((2, CHUNKS)), dma((2,)), dma((3,)), dma((2,)),
             dma((9, 12)), dma((9, 12)), dma((RING, MESSAGES)), dma((RING, MESSAGES)), dma((6,)), dma((6,)),
         ],
         compiler_params=pltpu.CompilerParams(
-            collective_id=1, has_side_effects=True, vmem_limit_bytes=VMEM_BYTES
+            collective_id=1, has_side_effects=True, vmem_limit_bytes=47 << 20
         ),
     )(lengths, inputs, cotangent, wq, w_out, w_in, w_down, *vectors)
 
 
 def widen_kernel(
     tiles, out_in, gin_in, sums, down, within, out, three, out_out, gin_out,
-    b_qv, b_out, gain1, shift1, b_in, b_down, gain2, shift2, low, wide, held, in_sem, out_sem, pass_sem,
+    b_qv, b_out, gain1, shift1, b_in, b_down, gain2, shift2, wide, out_sem, pass_sem,
 ):
-    enter = [pltpu.make_async_copy(ref, held.at[i], pass_sem.at[i]) for i, ref in enumerate((out_in, gin_in))]
-    leave = [pltpu.make_async_copy(held.at[i], ref, pass_sem.at[i]) for i, ref in enumerate((out_out, gin_out))]
-    loads = [pltpu.make_async_copy(tiles.at[k], low.at[k], in_sem.at[k]) for k in range(CHUNKS)]
-    for copy in loads[:RING] + enter + loads[RING:]:
+    leave = [pltpu.make_async_copy(ref, to, pass_sem.at[i]) for i, (ref, to) in enumerate(((out_in, out_out), (gin_in, gin_out)))]
+    for copy in leave:
         copy.start()
     width, half = sums.shape[1], b_qv.shape[1]
     for ref, row in ((gain1, 0), (shift1, 1), (b_out, 2), (gain2, 3), (shift2, 4), (b_down, 5)):
@@ -926,19 +915,14 @@
 
     stores = [store(k) for k in range(CHUNKS)]
     for k in range(CHUNKS):
-        loads[k].wait()
         if k >= RING:
             stores[k - RING].wait()
         def body(i, _):
             r = span(i, 32)
-            wide[k % RING, r, :] = low[k, r, :].astype(F32)
+            wide[k % RING, r, :] = tiles[k, r, :].astype(F32)
             return 0
         lax.fori_loop(0, TILE // 32, body, 0)
         stores[k].start()
-        if k == RING:
-            for into, back in zip(enter, leave):
-                into.wait()
-                back.start()
     for copy in stores[CHUNKS - RING :] + leave:
         copy.wait()
 
@@ -954,12 +938,12 @@
             jax.ShapeDtypeStruct(output.shape, output.dtype), jax.ShapeDtypeStruct(output.shape, output.dtype),
             wide(2, half_width), wide(width), wide(width), wide(width), wide(half_hidden), wide(width), wide(width), wide(width),
         ],
-        in_specs=[anywhere] * 3 + [inside],
+        in_specs=[inside] * 4,
         out_specs=[anywhere] * 6 + [inside] * 8,
         scratch_shapes=[
-            vm((CHUNKS,) + tile, BF), vm((RING,) + tile, F32), vm((2,) + output.shape, BF), dma((CHUNKS,)), dma((RING,)), dma((2,)),
+            vm((RING,) + tile, F32), dma((RING,)), dma((2,)),
         ],
-        compiler_params=pltpu.CompilerParams(vmem_limit_bytes=60 << 20),
+        compiler_params=pltpu.CompilerParams(vmem_limit_bytes=16 << 20),
     )(tiles, output, grad_inputs, sums)
 
 

time: 266 us -> 256 us (0.962)
  Pallas kernels: 265 us -> 255 us
    pallas_call x1, Pallas kernels: 15.8 us -> 9.66 us  [widen(): pl.pallas_call(widen_kernel, out_shape=[wide(half_hidden, width), wide(wi...]
    pallas_call x1, Pallas kernels: 250 us -> 245 us  [layer(): pl.pallas_call(layer_kernel, out_shape=[pltpu.VMEM(inputs.shape, BF), plt...]
where the time goes in v4:
time: 256 us
  Pallas kernels  255 us (100%)
    pallas_call x1, Pallas kernels, layer(): pl.pallas_call(layer_kernel, out_shape=[pltpu.VMEM(inputs.shape, BF), plt...  245 us
    pallas_call x1, Pallas kernels, widen(): pl.pallas_call(widen_kernel, out_shape=[wide(half_hidden, width), wide(wi...  9.66 us

profile of v4, /device:TPU:0, one launch (start us, length us, event | category | flops | bytes accessed | tf_op | source)
XLA Modules:
  0.0 255.8 jit_solution(10762616688991690069)
XLA Ops:
  0.7 245.3 %shard_map.254 = (bf16[512,1024]{1,0:T(8,128)(2,1)S(1)}, bf16[512,1024]{1,0:T(8,128)(2,1)S(1)}, bf16[24,512,512]{2,1,0:T(8,128)(2,1)S(1)}, f32[16,1024]{1,0:T(8,...) custom-call(s32[2]{0:T(128)} %lengths.1, ...), custom_call_target="tpu_custom_call" | custom-call | tf_op jit(solution)/shard_map/pallas_call | solution.py:868
  245.9 9.7 %shard_map.255 = (f32[2048,1024]{1,0:T(8,128)}, f32[1024,2048]{1,0:T(8,128)}, f32[512,1024]{1,0:T(8,128)}, f32[3,1024,512]{2,1,0:T(8,128)}, bf16[512,1024]{1,0:T...) custom-call(bf16[24,512,512]{2,1,0:T(8,128)(2,1)S(1)} %get-tuple-ele, ...), custom_call_target="tpu_custom_call" | custom-call | tf_op jit(solution)/shard_map/pallas_call | solution.py:934

commit v5 on v4

--- a/solution.py
+++ b/solution.py
@@ -331,7 +331,7 @@
 CHUNKS = 24
 RING = 4
 BF, F32 = jnp.bfloat16, jnp.float32
-ROWS_AT_ONCE = 64
+ROWS_AT_ONCE = 128
 
 
 def dot(a, b, ca, cb):

time: 256 us -> 255 us (level)
  no operation moved by 1% of the time
where the time goes in v5:
time: 255 us
  Pallas kernels  254 us (100%)
    pallas_call x1, Pallas kernels, layer(): pl.pallas_call(layer_kernel, out_shape=[pltpu.VMEM(inputs.shape, BF), plt...  244 us
    pallas_call x1, Pallas kernels, widen(): pl.pallas_call(widen_kernel, out_shape=[wide(half_hidden, width), wide(wi...  9.66 us

profile of v5, /device:TPU:0, one launch (start us, length us, event | category | flops | bytes accessed | tf_op | source)
XLA Modules:
  0.0 255.0 jit_solution(10635054770892450117)
XLA Ops:
  0.7 244.5 %shard_map.254 = (bf16[512,1024]{1,0:T(8,128)(2,1)S(1)}, bf16[512,1024]{1,0:T(8,128)(2,1)S(1)}, bf16[24,512,512]{2,1,0:T(8,128)(2,1)S(1)}, f32[16,1024]{1,0:T(8,...) custom-call(s32[2]{0:T(128)} %lengths.1, ...), custom_call_target="tpu_custom_call" | custom-call | tf_op jit(solution)/shard_map/pallas_call | solution.py:868
  245.2 9.7 %shard_map.255 = (f32[2048,1024]{1,0:T(8,128)}, f32[1024,2048]{1,0:T(8,128)}, f32[512,1024]{1,0:T(8,128)}, f32[3,1024,512]{2,1,0:T(8,128)}, bf16[512,1024]{1,0:T...) custom-call(bf16[24,512,512]{2,1,0:T(8,128)(2,1)S(1)} %get-tuple-ele, ...), custom_call_target="tpu_custom_call" | custom-call | tf_op jit(solution)/shard_map/pallas_call | solution.py:934

commit v6 on v5

--- a/solution.py
+++ b/solution.py
@@ -684,8 +684,8 @@
         if s == 7:
             wait(k, (11,))
 
-    def reduce_step(t):
-        for s in range(8):
+    def reduce_step(t, stages):
+        for s in stages:
             @pl.when((t >= s) & (t - s < CHUNKS))
             def _():
                 reduce_stage(t - s, s)
@@ -796,7 +796,7 @@
             a = xv[:, span(j % 2, TILE)]
             own[t] = dot(a, qkv[0, j // 2], 0, 0).astype(BF)
             oth[t] = dot(a, qkv[1, j // 2], 0, 0).astype(BF)
-        reduce_step(t)
+        reduce_step(t, (0, 1, 2, 3))
         @pl.when(t < 8)
         def _():
             @pl.when(t < 7)
@@ -852,6 +852,7 @@
             @pl.when(t == 16 + i)
             def _():
                 small_step(i)
+        reduce_step(t, range(4, 8))
         return 0
 
     lax.fori_loop(0, CHUNKS + 7, iteration, 0)

time: 255 us -> 254 us (level)
  no operation moved by 1% of the time
where the time goes in v6:
time: 254 us
  Pallas kernels  253 us (100%)
    pallas_call x1, Pallas kernels, layer(): pl.pallas_call(layer_kernel, out_shape=[pltpu.VMEM(inputs.shape, BF), plt...  243 us
    pallas_call x1, Pallas kernels, widen(): pl.pallas_call(widen_kernel, out_shape=[wide(half_hidden, width), wide(wi...  9.66 us

profile of v6, /device:TPU:0, one launch (start us, length us, event | category | flops | bytes accessed | tf_op | source)
XLA Modules:
  0.0 253.7 jit_solution(14965700907257430543)
XLA Ops:
  0.7 243.2 %shard_map.254 = (bf16[512,1024]{1,0:T(8,128)(2,1)S(1)}, bf16[512,1024]{1,0:T(8,128)(2,1)S(1)}, bf16[24,512,512]{2,1,0:T(8,128)(2,1)S(1)}, f32[16,1024]{1,0:T(8,...) custom-call(s32[2]{0:T(128)} %lengths.1, ...), custom_call_target="tpu_custom_call" | custom-call | tf_op jit(solution)/shard_map/pallas_call | solution.py:869
  243.9 9.7 %shard_map.255 = (f32[2048,1024]{1,0:T(8,128)}, f32[1024,2048]{1,0:T(8,128)}, f32[512,1024]{1,0:T(8,128)}, f32[3,1024,512]{2,1,0:T(8,128)}, bf16[512,1024]{1,0:T...) custom-call(bf16[24,512,512]{2,1,0:T(8,128)(2,1)S(1)} %get-tuple-ele, ...), custom_call_target="tpu_custom_call" | custom-call | tf_op jit(solution)/shard_map/pallas_call | solution.py:935

commit v7 on v6

--- a/solution.py
+++ b/solution.py
@@ -413,7 +413,7 @@
 
     def gather_message(n, kind):
         size = arrays[n][0].shape[0] // 2
-        size_part = size // 8 - (8 if n >= 4 else 0)
+        size_part = size // 8 - (16 if n >= 4 else 0)
         near_a, near_b = 2 * zb, 4 + 2 * x
         far_a, far_b = 2 * (1 - zb), 4 + 2 * (1 - x)
         one_a, one_b = 2 * zb + x, 4 + 2 * x + zb

time: 254 us -> 251 us (0.988)
  Pallas kernels: 253 us -> 250 us
    pallas_call x1, Pallas kernels: 243 us -> 240 us  [layer(): pl.pallas_call(layer_kernel, out_shape=[pltpu.VMEM(inputs.shape, BF), plt...]
where the time goes in v7:
time: 251 us
  Pallas kernels  250 us (100%)
    pallas_call x1, Pallas kernels, layer(): pl.pallas_call(layer_kernel, out_shape=[pltpu.VMEM(inputs.shape, BF), plt...  240 us
    pallas_call x1, Pallas kernels, widen(): pl.pallas_call(widen_kernel, out_shape=[wide(half_hidden, width), wide(wi...  9.66 us

profile of v7, /device:TPU:0, one launch (start us, length us, event | category | flops | bytes accessed | tf_op | source)
XLA Modules:
  0.0 250.5 jit_solution(7069910884343413213)
XLA Ops:
  0.7 240.0 %shard_map.254 = (bf16[512,1024]{1,0:T(8,128)(2,1)S(1)}, bf16[512,1024]{1,0:T(8,128)(2,1)S(1)}, bf16[24,512,512]{2,1,0:T(8,128)(2,1)S(1)}, f32[16,1024]{1,0:T(8,...) custom-call(s32[2]{0:T(128)} %lengths.1, ...), custom_call_target="tpu_custom_call" | custom-call | tf_op jit(solution)/shard_map/pallas_call | solution.py:869
  240.7 9.7 %shard_map.255 = (f32[2048,1024]{1,0:T(8,128)}, f32[1024,2048]{1,0:T(8,128)}, f32[512,1024]{1,0:T(8,128)}, f32[3,1024,512]{2,1,0:T(8,128)}, bf16[512,1024]{1,0:T...) custom-call(bf16[24,512,512]{2,1,0:T(8,128)(2,1)S(1)} %get-tuple-ele, ...), custom_call_target="tpu_custom_call" | custom-call | tf_op jit(solution)/shard_map/pallas_call | solution.py:935

commit v8 on v7

--- a/solution.py
+++ b/solution.py
@@ -796,7 +796,7 @@
             a = xv[:, span(j % 2, TILE)]
             own[t] = dot(a, qkv[0, j // 2], 0, 0).astype(BF)
             oth[t] = dot(a, qkv[1, j // 2], 0, 0).astype(BF)
-        reduce_step(t, (0, 1, 2, 3))
+        reduce_step(t, (0, 1, 2))
         @pl.when(t < 8)
         def _():
             @pl.when(t < 7)
@@ -852,7 +852,7 @@
             @pl.when(t == 16 + i)
             def _():
                 small_step(i)
-        reduce_step(t, range(4, 8))
+        reduce_step(t, range(3, 8))
         return 0
 
     lax.fori_loop(0, CHUNKS + 7, iteration, 0)

time: 251 us -> 254 us (1.012)
  Pallas kernels: 250 us -> 253 us
    pallas_call x1, Pallas kernels: 240 us -> 243 us  [layer(): pl.pallas_call(layer_kernel, out_shape=[pltpu.VMEM(inputs.shape, BF), plt...]
where the time goes in v8:
time: 254 us
  Pallas kernels  253 us (100%)
    pallas_call x1, Pallas kernels, layer(): pl.pallas_call(layer_kernel, out_shape=[pltpu.VMEM(inputs.shape, BF), plt...  243 us
    pallas_call x1, Pallas kernels, widen(): pl.pallas_call(widen_kernel, out_shape=[wide(half_hidden, width), wide(wi...  9.66 us

profile of v8, /device:TPU:0, one launch (start us, length us, event | category | flops | bytes accessed | tf_op | source)
XLA Modules:
  0.0 253.9 jit_solution(15242009009377723630)
XLA Ops:
  0.7 243.4 %shard_map.254 = (bf16[512,1024]{1,0:T(8,128)(2,1)S(1)}, bf16[512,1024]{1,0:T(8,128)(2,1)S(1)}, bf16[24,512,512]{2,1,0:T(8,128)(2,1)S(1)}, f32[16,1024]{1,0:T(8,...) custom-call(s32[2]{0:T(128)} %lengths.1, ...), custom_call_target="tpu_custom_call" | custom-call | tf_op jit(solution)/shard_map/pallas_call | solution.py:869
  244.0 9.7 %shard_map.255 = (f32[2048,1024]{1,0:T(8,128)}, f32[1024,2048]{1,0:T(8,128)}, f32[512,1024]{1,0:T(8,128)}, f32[3,1024,512]{2,1,0:T(8,128)}, bf16[512,1024]{1,0:T...) custom-call(bf16[24,512,512]{2,1,0:T(8,128)(2,1)S(1)} %get-tuple-ele, ...), custom_call_target="tpu_custom_call" | custom-call | tf_op jit(solution)/shard_map/pallas_call | solution.py:935
